TPU v7x, 512 devices: a whole 4x8x8 slice. The times are simulated.
512 devices in a mesh: chan: 32 (over y, x), row: 16 (over z, core).
Axes of the slice: x: 4, y: 8, z: 8, core: 2. Of those that a mesh axis runs over, the one named last changes fastest.
Arguments:
- amplitudes: bfloat16 [32, 3072, 2048], P('chan', 'row'), may hold values from -6 to 6
- interaction: bfloat16 [32, 2048, 2048], P('chan', 'row'), as said below
- weights6j: float32 [32, 2048], P('chan'), may hold values from -1.5 to 1.5
- column_order: int32 [32, 2048], P('chan'), may hold values from 0 to 2047, each once within a row
- row_counts: int32 [32], P('chan'), may hold values from 768 to 3072, as said below
Outputs:
- pp_update: bfloat16 [32, 3072, 2048], P('chan', 'row')
Inputs may be any that keep to these rules, and one draw needn't show every extreme that they name: Each channel's interaction block is symmetric. `row_counts`: some channel has all 3072 rows live and some channel exactly 768 in every draw.
All inputs are finite; a program needn't handle non-finite values.
Results may differ from a plain program's by a relative error of at most 0.005.
Values may be sent and summed in bfloat16 or wider, within the bound.
No kernel may reach another device: no remote copies, remote signals or barrier semaphores. Data moves between devices by JAX's collectives and lax.ppermute only.
A program may use at most 64 MiB of HBM per device.

v0:
```python
import jax
import jax.numpy as jnp
from jax import lax
from jax.sharding import PartitionSpec as P


def per_device(amplitudes, interaction, weights6j, column_order, row_counts):
    own_block = amplitudes[0]
    row_count = own_block.shape[0]
    col_count = own_block.shape[1]
    v_panel = interaction[0]
    col_order = column_order[0]
    col_weight = weights6j[0]
    gathered = lax.all_to_all(own_block, "chan", split_axis=1, concat_axis=1, tiled=True)
    row_start = lax.axis_index("row") * row_count
    live_rows = row_start + jnp.arange(row_count, dtype=jnp.int32) < row_counts[0]
    taken = jnp.take(gathered, col_order, axis=1).astype(jnp.float32) * col_weight[None, :]
    recoupled = jnp.where(live_rows[:, None], taken, jnp.float32(0.0)).astype(jnp.bfloat16)
    product = jnp.dot(
        recoupled,
        lax.all_gather(v_panel, "row", axis=0, tiled=True),
        preferred_element_type=jnp.float32,
    )
    scaled = (product * col_weight[None, :]).astype(jnp.bfloat16)
    inverse = (
        jnp.zeros((col_count,), jnp.int32).at[col_order].set(jnp.arange(col_count, dtype=jnp.int32))
    )
    restored = jnp.take(scaled, inverse, axis=1)
    returned = lax.all_to_all(restored, "chan", split_axis=1, concat_axis=1, tiled=True)
    return returned[None]


def solution(mesh):
    in_specs = (
        P("chan", "row", None),
        P("chan", "row", None),
        P("chan", None),
        P("chan", None),
        P("chan"),
    )
    out_specs = P("chan", "row", None)
    return jax.shard_map(
        per_device, mesh=mesh, in_specs=in_specs, out_specs=out_specs, check_vma=False
    )
```

profile of v0, /device:TPU:6, one launch (start us, length us, event | category | flops | bytes accessed | tf_op | source)
XLA Modules:
  0.0 133.4 jit_solution(3425176206983938947)
XLA Ops:
  6.5 0.0 all-gather.3.cloned.1.call-start
  6.5 0.7 all-gather.3.cloned.1.call-update
  7.3 0.0 copy-start
  7.3 2.3 %copy.10 = bf16[1,192,2048]{1,2,0:T(8,128)(2,1)} copy(bf16[1,192,2048]{2,1,0:T(8,128)(2,1)} %param.7) | data formatting | bytes 1572864 | tf_op args[0]
  9.5 10.2 %all-to-all-start = ((bf16[192,32,64]{0,2,1:T(8,128)(2,1)}), bf16[192,32,64]{0,2,1:T(8,128)(2,1)S(1)}, u32[]{:S(2)}, u32[]{:S(2)}) async-start(bf16[192,32,64]{0,2,1:T(8,128)(2,1)} %bitcast.4), calls=%async_computation | async-start | bytes 2097152 | tf_op jit(solution)/shard_map/all_to_all | solution.py:14
  20.4 0.0 copy-done
  20.4 8.0 %scatter_custom_fusion = s32[2048]{0:T(1024)S(1)} fusion(s32[2048]{0:T(1024)S(1)} %bitcast.30, s32[2048]{0:T(1024)S(1)} %iota.9, s32[]{:T(128)} %constant.4.clone.1), kind=kCustom, calls=%fused_computation.23 | custom fusion | bytes 8196 | tf_op jit(solution)/shard_map/scatter | solution.py:26
  28.5 19.2 %all-to-all-done = bf16[192,32,64]{0,2,1:T(8,128)(2,1)S(1)} async-done(((bf16[192,32,64]{0,2,1:T(8,128)(2,1)}), bf16[192,32,64]{0,2,1:T(8,128)(2,1)S(1)}, u32[]{:S(2)}, u32[]{:S(2)}) %all-to-all-start) | async-done | bytes 786464 | tf_op jit(solution)/shard_map/all_to_all | solution.py:14
  47.8 7.5 %gather_fusion = bf16[2048,192]{1,0:T(8,128)(2,1)S(1)} fusion(bf16[192,2048]{0,1:T(8,128)(2,1)S(1)} %bitcast.25, s32[2048]{0:T(1024)S(1)} %fusion.15), kind=kCustom, calls=%fused_computation.clone | custom fusion | bytes 1581056 | tf_op jit(solution)/shard_map/jit(_take)/gather | solution.py:17
  55.3 0.0 copy-start.1
  55.3 0.5 copy.11
  55.8 17.6 %all-gather.3.cloned.1.call-done = bf16[1,2048,2048]{2,1,0:T(8,128)(2,1)} async-done(((bf16[1,128,2048]{2,1,0:T(8,128)(2,1)}), bf16[1,2048,2048]{2,1,0:T(8,128)(2,1)}) %all-gather.3.cloned.1.call-update) | async-done | bytes 8388624 | tf_op jit(solution)/shard_map/all_gather | solution.py:21
  73.4 0.0 copy-done.1
  73.4 5.2 %fusion.5 = bf16[192,2048]{1,0:T(8,128)(2,1)S(1)} fusion(bf16[1,2048,2048]{2,1,0:T(8,128)(2,1)} %all-gather.3.cloned.1.call-done, bf16[2048,192]{0,1:T(8,128)(2,1)S(1)} %copy.11, f32[2048]{0:T(1024)S(1)} %bitcast.31, pred[192]{0:T(512)(128)(4,1)S(1)} %add_compare_fusion, pred[2048]{0:T(1024)(128)(4,1)S(1)} %compare_and_fusion.1), kind=kOutput, calls=%fused_computation.6 | convolution fusion | flops 1613365248 | bytes 9971904 | tf_op jit(solution)/shard_map/dot_general | solution.py:19
  78.7 0.5 copy.12
  79.2 7.5 %gather_fusion.1 = bf16[2048,192]{1,0:T(8,128)(2,1)S(1)} fusion(bf16[192,2048]{0,1:T(8,128)(2,1)S(1)} %copy.12, s32[2048]{0:T(1024)S(1)} %fusion.16), kind=kCustom, calls=%fused_computation.1.clone | custom fusion | bytes 1581056 | tf_op jit(solution)/shard_map/jit(_take)/gather | solution.py:28
  86.7 0.4 broadcast_select_fusion
  87.2 38.1 %all_to_all.21 = bf16[192,32,64]{0,2,1:T(8,128)(2,1)S(1)} all-to-all(bf16[192,32,64]{0,2,1:T(8,128)(2,1)S(1)} %bitcast.26), channel_id=1, replica_groups=mesh['chan'=32,'row'=16] {'chan'}, dimensions={1} | all-to-all | bytes 1572864 | tf_op jit(solution)/shard_map/all_to_all | solution.py:29
  125.3 1.2 copy.13
  (7 shorter events, 0.1 us)
Async XLA Ops:
  6.5 66.9 %all-gather.3.cloned.1.call-start = ((), (), s32[]{:S(2)}) async-start(), calls=%async_computation.2 | async-start | bytes 8912896 | tf_op jit(solution)/shard_map/all_gather | solution.py:21
  7.3 13.1 %copy-start = (s32[1,2048]{1,0:T(1,128)S(1)}, s32[1,2048]{1,0:T(1,128)}, u32[]{:S(2)}) copy-start(s32[1,2048]{1,0:T(1,128)} %param.10) | copy-start | bytes 24580
  9.5 38.3 %all-to-all-start = ((bf16[192,32,64]{0,2,1:T(8,128)(2,1)}), bf16[192,32,64]{0,2,1:T(8,128)(2,1)S(1)}, u32[]{:S(2)}, u32[]{:S(2)}) async-start(bf16[192,32,64]{0,2,1:T(8,128)(2,1)} %bitcast.4), calls=%async_computation | async-start | bytes 2097152 | tf_op jit(solution)/shard_map/all_to_all | solution.py:14
  55.3 18.2 %copy-start.1 = (f32[1,2048]{1,0:T(1,128)S(1)}, f32[1,2048]{1,0:T(1,128)}, u32[]{:S(2)}) copy-start(f32[1,2048]{1,0:T(1,128)} %param.9) | copy-start | bytes 24580
Sparse Core Ops, SparseCore 0:
  9.5 63.9 all-gather.2
where the time goes:
time: 134 us; the launch traced here: 133 us
  blocking collectives  38.1 us (28%)
  waiting for transfers between devices  37.6 us (28%)
  local copies, waits for them, and re-layouts  27.6 us (21%)
  between operations  14.2 us (11%)
  starting transfers between devices  10.2 us (8%)
  matrix products  5.22 us (4%)
    all_to_all x1, blocking collectives, per_device(): lax.all_to_all(restored, 'chan', split_axis=1, concat_axis=1, tiled=True)  38.1 us
    all_to_all x1, waiting for transfers between devices, per_device(): lax.all_to_all(own_block, 'chan', split_axis=1, concat_axis=1, tiled=True)  19.2 us
    all_gather x1, waiting for transfers between devices, per_device(): lax.all_gather(v_panel, 'row', axis=0, tiled=True)  17.6 us
    all_to_all x1, starting transfers between devices, per_device(): lax.all_to_all(own_block, 'chan', split_axis=1, concat_axis=1, tiled=True)  10.2 us
    scatter x1, local copies, waits for them, and re-layouts, per_device(): jnp.zeros((col_count,), jnp.int32).at[col_order]  8.05 us
    gather x2, local copies, waits for them, and re-layouts, per_device(): jnp.take(gathered, col_order, axis=1).astype(jnp.float32)  7.99 us
    gather x1, local copies, waits for them, and re-layouts, per_device(): restored = jnp.take(scaled, inverse, axis=1)  7.5 us
    dot_general x1, matrix products, per_device(): jnp.dot(recoupled, lax.all_gather(v_panel, 'row', axis=0, tiled=True), pr...  5.22 us
  transfers between devices with their start and end apart: 2, of which 2 were waited for; matrix products, arithmetic and copies ran while one was open for 14% of the time, Pallas kernels for 0%

commit v1 on v0

v1 whole, which is shorter than its diff:
```python
import jax
import jax.numpy as jnp
from jax import lax
from jax.experimental import pallas as pl
from jax.experimental.pallas import tpu as pltpu
from jax.sharding import PartitionSpec as P

VMEM_LIMIT = 56 * 1024 * 1024
TILE = 256


def call(body, out_shape, in_specs, scratch=()):
    return pl.pallas_call(
        body,
        out_shape=out_shape,
        in_specs=in_specs,
        out_specs=pl.BlockSpec(memory_space=pltpu.VMEM),
        scratch_shapes=list(scratch),
        compiler_params=pltpu.CompilerParams(vmem_limit_bytes=VMEM_LIMIT),
    )


def vmem():
    return pl.BlockSpec(memory_space=pltpu.VMEM)


def smem():
    return pl.BlockSpec(memory_space=pltpu.SMEM)


def anywhere():
    return pl.BlockSpec(memory_space=pl.ANY)


def swap_halves(upper, lower):
    low_lane = lax.broadcasted_iota(jnp.int32, upper.shape, 1) < 64
    first = jnp.where(low_lane, upper, pltpu.roll(lower, 64, 1))
    second = jnp.where(low_lane, pltpu.roll(upper, 64, 1), lower)
    return first, second


def pack_body(block_ref, out_ref):
    half = block_ref.shape[0] // 2
    for pair in range(out_ref.shape[0] // 2):
        lanes = pl.ds(pair * 128, 128)
        first, second = swap_halves(
            block_ref[:half, lanes].astype(jnp.float32), block_ref[half:, lanes].astype(jnp.float32)
        )
        out_ref[2 * pair] = first.astype(out_ref.dtype)
        out_ref[2 * pair + 1] = second.astype(out_ref.dtype)


def unpack_body(groups_ref, out_ref):
    half = groups_ref.shape[1]
    for pair in range(groups_ref.shape[0] // 2):
        lanes = pl.ds(pair * 128, 128)
        upper, lower = swap_halves(
            groups_ref[2 * pair].astype(jnp.float32), groups_ref[2 * pair + 1].astype(jnp.float32)
        )
        out_ref[:half, lanes] = upper.astype(out_ref.dtype)
        out_ref[half:, lanes] = lower.astype(out_ref.dtype)


def selection(order, first):
    rows = lax.broadcasted_iota(jnp.int32, (TILE, order.shape[1]), 0) + first
    return jnp.where(rows == order, 1.0, 0.0).astype(jnp.bfloat16)


def recouple_body(live_ref, groups_ref, order_ref, weight_ref, out_ref, gathered):
    unpack_body(groups_ref, gathered)
    row_count, col_count = out_ref.shape
    live = lax.broadcasted_iota(jnp.int32, (row_count, TILE), 0) < live_ref[0]
    for at in range(0, col_count, TILE):
        order = order_ref[:, at : at + TILE]
        rows = lax.broadcasted_iota(jnp.int32, (col_count, TILE), 0)
        picks = jnp.where(rows == order, 1.0, 0.0).astype(jnp.bfloat16)
        taken = jnp.dot(gathered[...], picks, preferred_element_type=jnp.float32)
        taken = taken * weight_ref[:, at : at + TILE]
        out_ref[:, at : at + TILE] = jnp.where(live, taken, 0.0).astype(out_ref.dtype)


def product_body(
    recoupled_ref, panel_ref, order_ref, weight_ref, out_ref, panel, scaled, restored, sems
):
    col_count = recoupled_ref.shape[1]
    steps = col_count // TILE
    copies = [
        pltpu.make_async_copy(
            panel_ref.at[:, pl.ds(step * TILE, TILE)], panel.at[step], sems.at[step]
        )
        for step in range(steps)
    ]
    for copy in copies:
        copy.start()
    for step in range(steps):
        at = step * TILE
        copies[step].wait()
        product = jnp.dot(recoupled_ref[...], panel[step], preferred_element_type=jnp.float32)
        scaled[:, at : at + TILE] = (product * weight_ref[:, at : at + TILE]).astype(scaled.dtype)
    for step in range(steps):
        at = step * TILE
        picks = selection(order_ref[...], at)
        placed = lax.dot_general(
            scaled[...], picks, (((1,), (1,)), ((), ())), preferred_element_type=jnp.float32
        )
        restored[:, at : at + TILE] = placed.astype(restored.dtype)
    pack_body(restored, out_ref)


def per_device(amplitudes, interaction, weights6j, column_order, row_counts):
    own_block = amplitudes[0]
    row_count, col_count = own_block.shape
    chan_count = lax.axis_size("chan")
    dtype = own_block.dtype
    packed_shape = (chan_count, row_count // 2, 128)
    packed = jax.ShapeDtypeStruct(packed_shape, dtype)
    flat = jax.ShapeDtypeStruct((row_count, col_count), dtype)
    steps = col_count // TILE

    v_panel = lax.all_gather(interaction[0], "row", axis=0, tiled=True)
    sent = call(pack_body, packed, [vmem()])(own_block)
    groups = lax.all_to_all(sent, "chan", split_axis=0, concat_axis=0, tiled=True)
    live_rows = row_counts - lax.axis_index("row") * row_count
    recoupled = call(
        recouple_body, flat, [smem(), vmem(), vmem(), vmem()], [pltpu.VMEM(flat.shape, dtype)]
    )(live_rows, groups, column_order, weights6j)
    restored = call(
        product_body,
        packed,
        [vmem(), anywhere(), vmem(), vmem()],
        [
            pltpu.VMEM((steps, col_count, TILE), dtype),
            pltpu.VMEM(flat.shape, dtype),
            pltpu.VMEM(flat.shape, dtype),
            pltpu.SemaphoreType.DMA((steps,)),
        ],
    )(recoupled, v_panel, column_order, weights6j)
    returned = lax.all_to_all(restored, "chan", split_axis=0, concat_axis=0, tiled=True)
    return call(unpack_body, flat, [vmem()])(returned)[None]


def solution(mesh):
    in_specs = (
        P("chan", "row", None),
        P("chan", "row", None),
        P("chan", None),
        P("chan", None),
        P("chan"),
    )
    out_specs = P("chan", "row", None)
    return jax.shard_map(
        per_device, mesh=mesh, in_specs=in_specs, out_specs=out_specs, check_vma=False
    )
```

time: 134 us -> 126 us (0.940)
  local copies, waits for them, and re-layouts: 27.6 us -> 0.88 us
  Pallas kernels: 0 us -> 19.9 us
  waiting for transfers between devices: 37.6 us -> 47.9 us
  blocking collectives: 38.1 us -> 32.8 us
  matrix products: 5.22 us -> 0 us
    pallas_call x0 -> x4, Pallas kernels: none -> 19.9 us  [the longest x1 10.3 us: per_device(): call(product_body, packed, [vmem(), anywhere(), vmem(), vmem()], [pltpu.V...]
    gather x3 -> x0, local copies, waits for them, and re-layouts: 15.5 us -> none  [the longest x2 7.99 us: per_device(): jnp.take(gathered, col_order, axis=1).astype(jnp.float32)]
    scatter x1 -> x0, local copies, waits for them, and re-layouts: 8.05 us -> none  [per_device(): jnp.zeros((col_count,), jnp.int32).at[col_order]]
    all_gather x1, waiting for transfers between devices: 17.6 us -> 25.4 us  [per_device(): v_panel = lax.all_gather(interaction[0], 'row', axis=0, tiled=True)]
    all_to_all x1, blocking collectives: 38.1 us -> 32.8 us  [per_device(): lax.all_to_all(restored, 'chan', split_axis=0, concat_axis=0, tiled=True)]
    dot_general x1 -> x0, matrix products: 5.22 us -> none  [per_device(): jnp.dot(recoupled, lax.all_gather(v_panel, 'row', axis=0, tiled=True), pr...]
    all_to_all x1, waiting for transfers between devices: 19.2 us -> 21.8 us  [per_device(): lax.all_to_all(sent, 'chan', split_axis=0, concat_axis=0, tiled=True)]
    unnamed x5 -> x2, local copies, waits for them, and re-layouts: 2.27 us -> 0.88 us
  transfers between devices with their start and end apart: 2 -> 2, of which waited for: 2 -> 2; matrix products, arithmetic and copies ran while one was open for 14% -> 0% of each run, Pallas kernels for 0% -> 6%
where the time goes in v1:
time: 126 us
  waiting for transfers between devices  47.9 us (38%)
  blocking collectives  32.8 us (26%)
  Pallas kernels  19.9 us (16%)
  between operations  14.1 us (11%)
  starting transfers between devices  10.2 us (8%)
    all_to_all x1, blocking collectives, per_device(): lax.all_to_all(restored, 'chan', split_axis=0, concat_axis=0, tiled=True)  32.8 us
    all_gather x1, waiting for transfers between devices, per_device(): v_panel = lax.all_gather(interaction[0], 'row', axis=0, tiled=True)  25.4 us
    all_to_all x1, waiting for transfers between devices, per_device(): lax.all_to_all(sent, 'chan', split_axis=0, concat_axis=0, tiled=True)  21.8 us
    pallas_call x1, Pallas kernels, per_device(): call(product_body, packed, [vmem(), anywhere(), vmem(), vmem()], [pltpu.V...  10.3 us
    all_to_all x1, starting transfers between devices, per_device(): lax.all_to_all(sent, 'chan', split_axis=0, concat_axis=0, tiled=True)  10.2 us
    pallas_call x1, Pallas kernels, per_device(): call(recouple_body, flat, [smem(), vmem(), vmem(), vmem()], [pltpu.VMEM(f...  4.92 us
  transfers between devices with their start and end apart: 2, of which 2 were waited for; matrix products, arithmetic and copies ran while one was open for 0% of the time, Pallas kernels for 6%

profile of v1, /device:TPU:6, one launch (start us, length us, event | category | flops | bytes accessed | tf_op | source)
XLA Modules:
  0.0 125.8 jit_solution(15211396862140359927)
XLA Ops:
  6.5 0.0 all-gather.3.cloned.1.call-start
  6.5 0.7 all-gather.3.cloned.1.call-update
  7.3 2.3 %shard_map.55 = bf16[32,96,128]{2,1,0:T(8,128)(2,1)} custom-call(bf16[192,2048]{1,0:T(8,128)(2,1)} %bitcast.5), custom_call_target="tpu_custom_call" | custom-call | tf_op jit(solution)/shard_map/pallas_call | solution.py:121
  9.6 10.2 %all-to-all-start = ((bf16[32,96,128]{2,1,0:T(8,128)(2,1)}), bf16[32,96,128]{2,1,0:T(8,128)(2,1)S(1)}, u32[]{:S(2)}, u32[]{:S(2)}) async-start(bf16[32,96,128]{2,1,0:T(8,128)(2,1)} %shard_map.55), calls=%async_computation | async-start | bytes 1572864 | tf_op jit(solution)/shard_map/all_to_all | solution.py:122
  20.4 21.8 %all-to-all-done.groups_ref = bf16[32,96,128]{2,1,0:T(8,128)(2,1)S(1)} async-done(((bf16[32,96,128]{2,1,0:T(8,128)(2,1)}), bf16[32,96,128]{2,1,0:T(8,128)(2,1)S(1)}, u32[]{:S(2)}, u32[]{:S(2)}) %all-to-all-start) | async-done | bytes 786464 | tf_op jit(solution)/shard_map/all_to_all | solution.py:122
  42.2 0.0 copy-start
  42.2 0.9 copy-done
  43.1 4.9 %shard_map.56.recoupled_ref = bf16[192,2048]{1,0:T(8,128)(2,1)} custom-call(s32[1]{0:T(128)S(6)} %sub.7.live_ref, bf16[32,96,128]{2,1,0:T(8,128)(2,1)} %copy-done, s32[1,2048]{1,0:T(1,128)} %order_ref.3, f32[1,2048]{1,0:T(1,128)} %weight_ref.3), custom_call_target="tpu_custom_call" | custom-call | tf_op jit(solution)/shard_map/pallas_call | solution.py:124
  48.0 25.4 %all-gather.3.cloned.1.call-done = bf16[1,2048,2048]{2,1,0:T(8,128)(2,1)} async-done(((bf16[1,128,2048]{2,1,0:T(8,128)(2,1)}), bf16[1,2048,2048]{2,1,0:T(8,128)(2,1)}) %all-gather.3.cloned.1.call-update) | async-done | bytes 8388624 | tf_op jit(solution)/shard_map/all_gather | solution.py:120
  73.4 10.3 %shard_map.57 = bf16[32,96,128]{2,1,0:T(8,128)(2,1)} custom-call(bf16[192,2048]{1,0:T(8,128)(2,1)} %shard_map.56.recoupled_ref, bf16[2048,2048]{1,0:T(8,128)(2,1)} %bitcast.4, s32[1,2048]{1,0:T(1,128)} %order_ref.3, f32[1,2048]{1,0:T(1,128)} %weight_ref.3), custom_call_target="tpu_custom_call" | custom-call | tf_op jit(solution)/shard_map/pallas_call | solution.py:127
  83.7 32.8 %all_to_all.10.groups_ref = bf16[32,96,128]{2,1,0:T(8,128)(2,1)} all-to-all(bf16[32,96,128]{2,1,0:T(8,128)(2,1)} %shard_map.57), channel_id=1, replica_groups=mesh['chan'=32,'row'=16] {'chan'}, dimensions={0} | all-to-all | bytes 1572864 | tf_op jit(solution)/shard_map/all_to_all | solution.py:138
  116.6 2.4 %shard_map.58 = bf16[192,2048]{1,0:T(8,128)(2,1)} custom-call(bf16[32,96,128]{2,1,0:T(8,128)(2,1)} %all_to_all.10.groups_ref), custom_call_target="tpu_custom_call" | custom-call | tf_op jit(solution)/shard_map/pallas_call | solution.py:139
Async XLA Ops:
  6.5 66.9 %all-gather.3.cloned.1.call-start = ((), (), s32[]{:S(2)}) async-start(), calls=%async_computation.2 | async-start | bytes 8912896 | tf_op jit(solution)/shard_map/all_gather | solution.py:120
  9.6 32.6 %all-to-all-start = ((bf16[32,96,128]{2,1,0:T(8,128)(2,1)}), bf16[32,96,128]{2,1,0:T(8,128)(2,1)S(1)}, u32[]{:S(2)}, u32[]{:S(2)}) async-start(bf16[32,96,128]{2,1,0:T(8,128)(2,1)} %shard_map.55), calls=%async_computation | async-start | bytes 1572864 | tf_op jit(solution)/shard_map/all_to_all | solution.py:122
  42.2 0.9 copy-start
Sparse Core Ops, SparseCore 0:
  9.5 63.9 all-gather.2

commit v2 on v1

--- a/solution.py
+++ b/solution.py
@@ -7,6 +7,7 @@
 
 VMEM_LIMIT = 56 * 1024 * 1024
 TILE = 256
+BLOCK = 128
 
 
 def call(body, out_shape, in_specs, scratch=()):
@@ -79,26 +80,51 @@
         out_ref[:, at : at + TILE] = jnp.where(live, taken, 0.0).astype(out_ref.dtype)
 
 
+def halve_body(start_ref, panel_ref, out_ref):
+    blocks = panel_ref.shape[1] // BLOCK
+    for step in range(out_ref.shape[1] // BLOCK):
+        at = pl.multiple_of((start_ref[0] + step) % blocks * BLOCK, BLOCK)
+        out_ref[:, step * BLOCK : (step + 1) * BLOCK] = panel_ref[:, pl.ds(at, BLOCK)]
+
+
 def product_body(
-    recoupled_ref, panel_ref, order_ref, weight_ref, out_ref, panel, scaled, restored, sems
+    recoupled_ref, halves_ref, order_ref, weight_ref, out_ref, panel, scaled, restored, sems
 ):
     col_count = recoupled_ref.shape[1]
-    steps = col_count // TILE
-    copies = [
-        pltpu.make_async_copy(
-            panel_ref.at[:, pl.ds(step * TILE, TILE)], panel.at[step], sems.at[step]
+    blocks, width = col_count // BLOCK, halves_ref.shape[1]
+    copies = []
+    for block in range(blocks):
+        rows = pl.ds(block * BLOCK, BLOCK)
+        inside = min(width, col_count - block * BLOCK)
+        parts = [(0, block * BLOCK, inside)]
+        if inside < width:
+            parts.append((inside, 0, width - inside))
+        copies.append(
+            [
+                pltpu.make_async_copy(
+                    halves_ref.at[rows, pl.ds(source, size)],
+                    panel.at[rows, pl.ds(target, size)],
+                    sems.at[2 * block + part],
+                )
+                for part, (source, target, size) in enumerate(parts)
+            ]
         )
-        for step in range(steps)
-    ]
-    for copy in copies:
-        copy.start()
-    for step in range(steps):
-        at = step * TILE
-        copies[step].wait()
-        product = jnp.dot(recoupled_ref[...], panel[step], preferred_element_type=jnp.float32)
+        for copy in copies[-1]:
+            copy.start()
+    for block in range(blocks):
+        for copy in copies[block]:
+            copy.wait()
+        own = slice(block * BLOCK, (block + 1) * BLOCK)
+        for step in range(1, blocks - width // BLOCK + 1):
+            other = (block + step) % blocks
+            there = slice(other * BLOCK, (other + 1) * BLOCK)
+            panel[there, own] = panel[own, there].T
+    for at in range(0, col_count, TILE):
+        product = jnp.dot(
+            recoupled_ref[...], panel[:, at : at + TILE], preferred_element_type=jnp.float32
+        )
         scaled[:, at : at + TILE] = (product * weight_ref[:, at : at + TILE]).astype(scaled.dtype)
-    for step in range(steps):
-        at = step * TILE
+    for at in range(0, col_count, TILE):
         picks = selection(order_ref[...], at)
         placed = lax.dot_general(
             scaled[...], picks, (((1,), (1,)), ((), ())), preferred_element_type=jnp.float32
@@ -115,12 +141,15 @@
     packed_shape = (chan_count, row_count // 2, 128)
     packed = jax.ShapeDtypeStruct(packed_shape, dtype)
     flat = jax.ShapeDtypeStruct((row_count, col_count), dtype)
-    steps = col_count // TILE
+    blocks = col_count // BLOCK
 
-    v_panel = lax.all_gather(interaction[0], "row", axis=0, tiled=True)
+    row_at = lax.axis_index("row")
+    half = jax.ShapeDtypeStruct((BLOCK, (blocks // 2 + 1) * BLOCK), dtype)
+    own_half = call(halve_body, half, [smem(), vmem()])(row_at[None], interaction[0])
+    halves = lax.all_gather(own_half, "row", axis=0, tiled=True)
     sent = call(pack_body, packed, [vmem()])(own_block)
     groups = lax.all_to_all(sent, "chan", split_axis=0, concat_axis=0, tiled=True)
-    live_rows = row_counts - lax.axis_index("row") * row_count
+    live_rows = row_counts - row_at * row_count
     recoupled = call(
         recouple_body, flat, [smem(), vmem(), vmem(), vmem()], [pltpu.VMEM(flat.shape, dtype)]
     )(live_rows, groups, column_order, weights6j)
@@ -129,12 +158,12 @@
         packed,
         [vmem(), anywhere(), vmem(), vmem()],
         [
-            pltpu.VMEM((steps, col_count, TILE), dtype),
+            pltpu.VMEM((col_count, col_count), dtype),
             pltpu.VMEM(flat.shape, dtype),
             pltpu.VMEM(flat.shape, dtype),
-            pltpu.SemaphoreType.DMA((steps,)),
+            pltpu.SemaphoreType.DMA((2 * blocks,)),
         ],
-    )(recoupled, v_panel, column_order, weights6j)
+    )(recoupled, halves, column_order, weights6j)
     returned = lax.all_to_all(restored, "chan", split_axis=0, concat_axis=0, tiled=True)
     return call(unpack_body, flat, [vmem()])(returned)[None]
 

time: 126 us -> 113 us (0.90)
  waiting for transfers between devices: 47.9 us -> 32.8 us
  Pallas kernels: 19.9 us -> 21.4 us
    all_gather x1, waiting for transfers between devices: 25.4 us -> 11 us  [per_device(): halves = lax.all_gather(own_half, 'row', axis=0, tiled=True)]
    pallas_call x0 -> x1, Pallas kernels: none -> 1.83 us  [per_device(): call(halve_body, half, [smem(), vmem()])(row_at[None], interaction[0])]
where the time goes in v2:
time: 113 us; the launch traced here: 112 us
  waiting for transfers between devices  32.8 us (29%)
  blocking collectives  32.8 us (29%)
  Pallas kernels  21.4 us (19%)
  between operations  14.1 us (12%)
  starting transfers between devices  10.2 us (9%)
    all_to_all x1, blocking collectives, per_device(): lax.all_to_all(restored, 'chan', split_axis=0, concat_axis=0, tiled=True)  32.8 us
    all_to_all x1, waiting for transfers between devices, per_device(): lax.all_to_all(sent, 'chan', split_axis=0, concat_axis=0, tiled=True)  21.8 us
    all_gather x1, waiting for transfers between devices, per_device(): halves = lax.all_gather(own_half, 'row', axis=0, tiled=True)  11 us
    all_to_all x1, starting transfers between devices, per_device(): lax.all_to_all(sent, 'chan', split_axis=0, concat_axis=0, tiled=True)  10.2 us
    pallas_call x1, Pallas kernels, per_device(): call(product_body, packed, [vmem(), anywhere(), vmem(), vmem()], [pltpu.V...  9.99 us
    pallas_call x1, Pallas kernels, per_device(): call(recouple_body, flat, [smem(), vmem(), vmem(), vmem()], [pltpu.VMEM(f...  4.89 us
    pallas_call x1, Pallas kernels, per_device(): return call(unpack_body, flat, [vmem()])(returned)[None]  2.35 us
    pallas_call x1, Pallas kernels, per_device(): sent = call(pack_body, packed, [vmem()])(own_block)  2.34 us
  transfers between devices with their start and end apart: 2, of which 2 were waited for; matrix products, arithmetic and copies ran while one was open for 0% of the time, Pallas kernels for 6%

profile of v2, /device:TPU:6, one launch (start us, length us, event | category | flops | bytes accessed | tf_op | source)
XLA Modules:
  0.0 112.2 jit_solution(2138753553355765027)
XLA Ops:
  6.5 0.0 all-gather.2.cloned.1.call-start
  6.5 1.8 %shard_map.57 = bf16[128,1152]{1,0:T(8,128)(2,1)} custom-call(s32[1]{0:T(128)} %bitcast.2.start_ref, bf16[128,2048]{1,0:T(8,128)(2,1)} %bitcast.6), custom_call_target="tpu_custom_call" | custom-call | tf_op jit(solution)/shard_map/pallas_call | solution.py:148
  8.4 0.0 all-gather.2.cloned.1.call-update
  8.4 2.3 %shard_map.55 = bf16[32,96,128]{2,1,0:T(8,128)(2,1)} custom-call(bf16[192,2048]{1,0:T(8,128)(2,1)} %bitcast.5), custom_call_target="tpu_custom_call" | custom-call | tf_op jit(solution)/shard_map/pallas_call | solution.py:150
  10.7 10.2 %all-to-all-start = ((bf16[32,96,128]{2,1,0:T(8,128)(2,1)}), bf16[32,96,128]{2,1,0:T(8,128)(2,1)S(1)}, u32[]{:S(2)}, u32[]{:S(2)}) async-start(bf16[32,96,128]{2,1,0:T(8,128)(2,1)} %shard_map.55), calls=%async_computation | async-start | bytes 1572864 | tf_op jit(solution)/shard_map/all_to_all | solution.py:151
  21.6 21.8 %all-to-all-done.groups_ref = bf16[32,96,128]{2,1,0:T(8,128)(2,1)S(1)} async-done(((bf16[32,96,128]{2,1,0:T(8,128)(2,1)}), bf16[32,96,128]{2,1,0:T(8,128)(2,1)S(1)}, u32[]{:S(2)}, u32[]{:S(2)}) %all-to-all-start) | async-done | bytes 786464 | tf_op jit(solution)/shard_map/all_to_all | solution.py:151
  43.4 0.0 copy-start
  43.4 0.9 copy-done
  44.3 4.9 %shard_map.56.recoupled_ref = bf16[192,2048]{1,0:T(8,128)(2,1)} custom-call(s32[1]{0:T(128)S(6)} %sub.7.live_ref, bf16[32,96,128]{2,1,0:T(8,128)(2,1)} %copy-done, s32[1,2048]{1,0:T(1,128)} %order_ref.3, f32[1,2048]{1,0:T(1,128)} %weight_ref.3), custom_call_target="tpu_custom_call" | custom-call | tf_op jit(solution)/shard_map/pallas_call | solution.py:153
  49.1 11.0 %all-gather.2.cloned.1.call-done.halves_ref = bf16[2048,1152]{1,0:T(8,128)(2,1)} async-done(((bf16[128,1152]{1,0:T(8,128)(2,1)}), bf16[2048,1152]{1,0:T(8,128)(2,1)}) %all-gather.2.cloned.1.call-update) | async-done | bytes 4718608 | tf_op jit(solution)/shard_map/all_gather | solution.py:149
  60.2 10.0 %shard_map.58 = bf16[32,96,128]{2,1,0:T(8,128)(2,1)} custom-call(bf16[192,2048]{1,0:T(8,128)(2,1)} %shard_map.56.recoupled_ref, bf16[2048,1152]{1,0:T(8,128)(2,1)} %all-gather.2.cloned.1.call-done.halves_ref, s32[1,2048]{1,0:T(1,128)} %order_ref.3, f32[1,2048]{1,0:T(1,128)} %weight_ref.3), custom_call_target="tpu_custom_call" | custom-call | tf_op jit(solution)/shard_map/pallas_call | solution.py:156
  70.2 32.8 %all_to_all.10.groups_ref = bf16[32,96,128]{2,1,0:T(8,128)(2,1)} all-to-all(bf16[32,96,128]{2,1,0:T(8,128)(2,1)} %shard_map.58), channel_id=1, replica_groups=mesh['chan'=32,'row'=16] {'chan'}, dimensions={0} | all-to-all | bytes 1572864 | tf_op jit(solution)/shard_map/all_to_all | solution.py:167
  103.0 2.4 %shard_map.59 = bf16[192,2048]{1,0:T(8,128)(2,1)} custom-call(bf16[32,96,128]{2,1,0:T(8,128)(2,1)} %all_to_all.10.groups_ref), custom_call_target="tpu_custom_call" | custom-call | tf_op jit(solution)/shard_map/pallas_call | solution.py:168
Async XLA Ops:
  6.5 53.6 %all-gather.2.cloned.1.call-start = ((), (), s32[]{:S(2)}) async-start(), calls=%async_computation.2 | async-start | bytes 5013504 | tf_op jit(solution)/shard_map/all_gather | solution.py:149
  10.7 32.6 %all-to-all-start = ((bf16[32,96,128]{2,1,0:T(8,128)(2,1)}), bf16[32,96,128]{2,1,0:T(8,128)(2,1)S(1)}, u32[]{:S(2)}, u32[]{:S(2)}) async-start(bf16[32,96,128]{2,1,0:T(8,128)(2,1)} %shard_map.55), calls=%async_computation | async-start | bytes 1572864 | tf_op jit(solution)/shard_map/all_to_all | solution.py:151
  43.4 0.9 copy-start
Sparse Core Ops, SparseCore 0:
  9.5 50.6 all-gather.1

commit v3 on v2

--- a/solution.py
+++ b/solution.py
@@ -5,7 +5,7 @@
 from jax.experimental.pallas import tpu as pltpu
 from jax.sharding import PartitionSpec as P
 
-VMEM_LIMIT = 56 * 1024 * 1024
+VMEM_LIMIT = 28 * 1024 * 1024
 TILE = 256
 BLOCK = 128
 
@@ -15,10 +15,14 @@
         body,
         out_shape=out_shape,
         in_specs=in_specs,
-        out_specs=pl.BlockSpec(memory_space=pltpu.VMEM),
+        out_specs=jax.tree.map(lambda _: vmem(), out_shape),
         scratch_shapes=list(scratch),
         compiler_params=pltpu.CompilerParams(vmem_limit_bytes=VMEM_LIMIT),
     )
+
+
+def near_core(array):
+    return pltpu.with_memory_space_constraint(array, pltpu.VMEM)
 
 
 def vmem():
@@ -80,40 +84,56 @@
         out_ref[:, at : at + TILE] = jnp.where(live, taken, 0.0).astype(out_ref.dtype)
 
 
-def halve_body(start_ref, panel_ref, out_ref):
+def rotated(table_ref, first, out_ref):
+    blocks = out_ref.shape[1] // BLOCK
+    for step in range(blocks):
+        at = pl.multiple_of((first + step) % blocks * BLOCK, BLOCK)
+        out_ref[:, step * BLOCK : (step + 1) * BLOCK] = table_ref[:, pl.ds(at, BLOCK)]
+
+
+def halve_body(row_ref, panel_ref, out_ref):
     blocks = panel_ref.shape[1] // BLOCK
     for step in range(out_ref.shape[1] // BLOCK):
-        at = pl.multiple_of((start_ref[0] + step) % blocks * BLOCK, BLOCK)
+        at = pl.multiple_of((row_ref[0] + step) % blocks * BLOCK, BLOCK)
         out_ref[:, step * BLOCK : (step + 1) * BLOCK] = panel_ref[:, pl.ds(at, BLOCK)]
 
 
-def product_body(
-    recoupled_ref, halves_ref, order_ref, weight_ref, out_ref, panel, scaled, restored, sems
-):
-    col_count = recoupled_ref.shape[1]
-    blocks, width = col_count // BLOCK, halves_ref.shape[1]
-    copies = []
+def send_body(row_ref, block_ref, order_ref, weight_ref, out_ref, order_out, weight_out):
+    pack_body(block_ref, out_ref)
+    first = row_ref[0] - row_ref[0] % 2
+    rotated(order_ref, first, order_out)
+    rotated(weight_ref, first, weight_out)
+
+
+def stack_body(*refs):
+    pieces, out_ref = refs[:-1], refs[-1]
+    for number, piece in enumerate(pieces):
+        out_ref[number * BLOCK : (number + 1) * BLOCK] = piece[...]
+
+
+def product_body(core_ref, recoupled_ref, order_ref, weight_ref, own_ref, partner_ref, *refs):
+    row_count, col_count = recoupled_ref.shape
+    blocks = col_count // BLOCK
+    out_ref, panel, scaled, restored = refs
+    width = own_ref.shape[1]
+
+    def place(stack, parity):
+        for number, chip in enumerate(CHIPS):
+            first = (2 * (chip % (blocks // 2)) + parity) * BLOCK
+            inside = min(width, col_count - first)
+            source = slice(number * BLOCK, (number + 1) * BLOCK)
+            panel[first : first + BLOCK, first : first + inside] = stack[source, :inside]
+            if inside < width:
+                panel[first : first + BLOCK, : width - inside] = stack[source, inside:]
+
+    for parity in range(2):
+
+        @pl.when(core_ref[0] == parity)
+        def _(parity=parity):
+            place(own_ref, parity)
+            place(partner_ref, 1 - parity)
+
     for block in range(blocks):
-        rows = pl.ds(block * BLOCK, BLOCK)
-        inside = min(width, col_count - block * BLOCK)
-        parts = [(0, block * BLOCK, inside)]
-        if inside < width:
-            parts.append((inside, 0, width - inside))
-        copies.append(
-            [
-                pltpu.make_async_copy(
-                    halves_ref.at[rows, pl.ds(source, size)],
-                    panel.at[rows, pl.ds(target, size)],
-                    sems.at[2 * block + part],
-                )
-                for part, (source, target, size) in enumerate(parts)
-            ]
-        )
-        for copy in copies[-1]:
-            copy.start()
-    for block in range(blocks):
-        for copy in copies[block]:
-            copy.wait()
         own = slice(block * BLOCK, (block + 1) * BLOCK)
         for step in range(1, blocks - width // BLOCK + 1):
             other = (block + step) % blocks
@@ -131,6 +151,9 @@
         )
         restored[:, at : at + TILE] = placed.astype(restored.dtype)
     pack_body(restored, out_ref)
+
+
+CHIPS = (0, -1, 1, -2, 2, -3, 3, 4)
 
 
 def per_device(amplitudes, interaction, weights6j, column_order, row_counts):
@@ -144,28 +167,57 @@
     blocks = col_count // BLOCK
 
     row_at = lax.axis_index("row")
+    rows = lax.axis_size("row")
+    core = row_at % 2
     half = jax.ShapeDtypeStruct((BLOCK, (blocks // 2 + 1) * BLOCK), dtype)
     own_half = call(halve_body, half, [smem(), vmem()])(row_at[None], interaction[0])
-    halves = lax.all_gather(own_half, "row", axis=0, tiled=True)
-    sent = call(pack_body, packed, [vmem()])(own_block)
+
+    def hop(far):
+        return [(row, (row + 2 * far) % rows) for row in range(rows)]
+
+    swap = [(row, row ^ 1) for row in range(rows)]
+    sent, order, weight = call(
+        send_body,
+        (
+            packed,
+            jax.ShapeDtypeStruct(column_order.shape, column_order.dtype),
+            jax.ShapeDtypeStruct(weights6j.shape, weights6j.dtype),
+        ),
+        [smem(), vmem(), vmem(), vmem()],
+    )(row_at[None], own_block, column_order, weights6j)
+    from_below = [lax.ppermute(own_half, "row", hop(far)) for far in (1, 2)]
+    from_above = [lax.ppermute(own_half, "row", hop(-far)) for far in (1, 2)]
+    sent = near_core(sent)
     groups = lax.all_to_all(sent, "chan", split_axis=0, concat_axis=0, tiled=True)
+    third_below = lax.ppermute(from_below[1], "row", hop(1))
+    third_above = lax.ppermute(from_above[1], "row", hop(-1))
+    apart = list(zip(hop(2), hop(-2)))
+    passed = jnp.where(core == 0, from_below[1], from_above[1])
+    opposite = lax.ppermute(passed, "row", [pair[row % 2] for row, pair in enumerate(apart)])
     live_rows = row_counts - row_at * row_count
     recoupled = call(
         recouple_body, flat, [smem(), vmem(), vmem(), vmem()], [pltpu.VMEM(flat.shape, dtype)]
-    )(live_rows, groups, column_order, weights6j)
+    )(live_rows, near_core(groups), order, weight)
+    third_below, recoupled = lax.optimization_barrier((third_below, recoupled))
+    pieces = [own_half, from_below[0], from_above[0], from_below[1], from_above[1]]
+    pieces += [third_below, third_above, opposite]
+    stack_shape = jax.ShapeDtypeStruct((len(pieces) * BLOCK, half.shape[1]), dtype)
+    stack = call(stack_body, stack_shape, [vmem()] * len(pieces))(*map(near_core, pieces))
+    stack = near_core(stack)
+    partner = near_core(lax.ppermute(stack, "row", swap))
     restored = call(
         product_body,
         packed,
-        [vmem(), anywhere(), vmem(), vmem()],
+        [smem(), *[vmem()] * 5],
         [
             pltpu.VMEM((col_count, col_count), dtype),
             pltpu.VMEM(flat.shape, dtype),
             pltpu.VMEM(flat.shape, dtype),
-            pltpu.SemaphoreType.DMA((2 * blocks,)),
         ],
-    )(recoupled, halves, column_order, weights6j)
+    )(core[None], near_core(recoupled), order, weight, stack, partner)
+    restored = near_core(restored)
     returned = lax.all_to_all(restored, "chan", split_axis=0, concat_axis=0, tiled=True)
-    return call(unpack_body, flat, [vmem()])(returned)[None]
+    return call(unpack_body, flat, [vmem()])(near_core(returned))[None]
 
 
 def solution(mesh):

time: 113 us -> 108 us (0.956)
  starting transfers between devices: 10.2 us -> 40.6 us
  between operations: 14.1 us -> 0.8 us
  waiting for transfers between devices: 32.8 us -> 20.5 us
  Pallas kernels: 21.4 us -> 10.4 us
  local copies, waits for them, and re-layouts: 0.88 us -> 2.53 us
    ppermute x0 -> x8, starting transfers between devices: none -> 30.4 us  [the longest x2 17 us: per_device(): from_above = [lax.ppermute(own_half, 'row', hop(-far)) for far in (1, 2)]]
    all_to_all x1, waiting for transfers between devices: 21.8 us -> 0.01 us  [per_device(): lax.all_to_all(sent, 'chan', split_axis=0, concat_axis=0, tiled=True)]
    ppermute x0 -> x8, waiting for transfers between devices: none -> 20.5 us  [the longest x1 6.3 us: per_device(): lax.ppermute(passed, 'row', [pair[row % 2] for row, pair in enumerate(apa...]
    all_gather x1 -> x0, waiting for transfers between devices: 11 us -> none  [per_device(): halves = lax.all_gather(own_half, 'row', axis=0, tiled=True)]
    pallas_call x3 -> x4, Pallas kernels: 14.7 us -> 7.48 us  [the longest x1 4.87 us: per_device(): call(product_body, packed, [smem(), *[vmem()] * 5], [pltpu.VMEM((col_coun...]
    pallas_call x1, Pallas kernels: 4.89 us -> 2.87 us  [per_device(): call(recouple_body, flat, [smem(), vmem(), vmem(), vmem()], [pltpu.VMEM(f...]
    pallas_call x1, Pallas kernels: 1.83 us -> 0.09 us  [per_device(): call(halve_body, half, [smem(), vmem()])(row_at[None], interaction[0])]
    unnamed x2 -> x8, local copies, waits for them, and re-layouts: 0.88 us -> 2.53 us
  transfers between devices with their start and end apart: 2 -> 9, of which waited for: 2 -> 5; matrix products, arithmetic and copies ran while one was open for 0% -> 0% of each run, Pallas kernels for 6% -> 3%
where the time goes in v3:
time: 108 us; the launch traced here: 107 us
  starting transfers between devices  40.6 us (38%)
  blocking collectives  32.3 us (30%)
  waiting for transfers between devices  20.5 us (19%)
  Pallas kernels  10.4 us (10%)
  local copies, waits for them, and re-layouts  2.53 us (2%)
    all_to_all x1, blocking collectives, per_device(): lax.all_to_all(restored, 'chan', split_axis=0, concat_axis=0, tiled=True)  32.3 us
    ppermute x2, starting transfers between devices, per_device(): from_above = [lax.ppermute(own_half, 'row', hop(-far)) for far in (1, 2)]  17 us
    all_to_all x1, starting transfers between devices, per_device(): lax.all_to_all(sent, 'chan', split_axis=0, concat_axis=0, tiled=True)  10.2 us
    ppermute x1, waiting for transfers between devices, per_device(): lax.ppermute(passed, 'row', [pair[row % 2] for row, pair in enumerate(apa...  6.3 us
    pallas_call x1, Pallas kernels, per_device(): call(product_body, packed, [smem(), *[vmem()] * 5], [pltpu.VMEM((col_coun...  4.87 us
    ppermute x1, waiting for transfers between devices, per_device(): partner = near_core(lax.ppermute(stack, 'row', swap))  4.5 us
    ppermute x2, starting transfers between devices, per_device(): from_below = [lax.ppermute(own_half, 'row', hop(far)) for far in (1, 2)]  3.84 us
    ppermute x1, starting transfers between devices, per_device(): third_above = lax.ppermute(from_above[1], 'row', hop(-1))  3.79 us
  transfers between devices with their start and end apart: 9, of which 5 were waited for; matrix products, arithmetic and copies ran while one was open for 0% of the time, Pallas kernels for 3%

profile of v3, /device:TPU:6, one launch (start us, length us, event | category | flops | bytes accessed | tf_op | source)
XLA Modules:
  0.0 107.2 jit_solution(5445974260900351012)
XLA Ops:
  0.0 0.0 copy-start
  0.0 1.1 %copy-done = bf16[1,192,2048]{2,1,0:T(8,128)(2,1)S(1)} copy-done((bf16[1,192,2048]{2,1,0:T(8,128)(2,1)S(1)}, bf16[1,192,2048]{2,1,0:T(8,128)(2,1)}, u32[]{:S(2)}) %copy-start) | copy-done | bytes 786456
  1.1 0.0 copy-start.2
  1.1 0.7 copy-done.2
  1.8 0.0 copy-start.3
  1.8 0.7 copy-done.3
  2.5 0.0 copy-start.1
  2.5 1.2 %shard_map.56 = (bf16[32,96,128]{2,1,0:T(8,128)(2,1)}, s32[1,2048]{1,0:T(1,128)S(1)}, f32[1,2048]{1,0:T(1,128)S(1)}) custom-call(s32[1]{0:T(128)} %bitcast.1.row_ref, bf16[192,2048]{1,0:T(8,128)(2,1)S(1)} %bitcast.6, s32[1,2048]{1,0:T(1,128)S(1)} %copy-done.2, f32[1,2048]{1,0:T(1,128)S(1)} %copy-done.3), custom_call_target="tpu_custom_call" | custom-call | tf_op jit(solution)/shard_map/pallas_call | solution.py:179
  3.7 10.2 %all-to-all-start = ((bf16[32,96,128]{2,1,0:T(8,128)(2,1)}), bf16[32,96,128]{2,1,0:T(8,128)(2,1)S(1)}, u32[]{:S(2)}, u32[]{:S(2)}) async-start(bf16[32,96,128]{2,1,0:T(8,128)(2,1)} %get-tuple-element.10), calls=%async_computation | async-start | bytes 1572864 | tf_op jit(solution)/shard_map/all_to_all | solution.py:191
  13.9 0.0 copy-done.1
  14.0 0.1 shard_map.55.refs_0_
  14.1 10.9 %collective-permute-start.4 = (bf16[128,1152]{1,0:T(8,128)(2,1)S(1)}, bf16[128,1152]{1,0:T(8,128)(2,1)S(1)}, u32[]{:S(2)}, u32[]{:S(2)}) collective-permute-start(bf16[128,1152]{1,0:T(8,128)(2,1)S(1)} %shard_map.55.refs_0_), channel_id=1, source_target_pairs={{0,12},{1,13},{2,14},{3,15},{4,0},{5,1},{6,2},{7,3},{8,4},{9,5},{1... | collective-permute-start | bytes 884744 | tf_op jit(solution)/shard_map/ppermute | solution.py:189
  25.0 1.9 %collective-permute-start = (bf16[128,1152]{1,0:T(8,128)(2,1)S(1)}, bf16[128,1152]{1,0:T(8,128)(2,1)S(1)}, u32[]{:S(2)}, u32[]{:S(2)}) collective-permute-start(bf16[128,1152]{1,0:T(8,128)(2,1)S(1)} %shard_map.55.refs_0_), channel_id=1, source_target_pairs={{0,4},{1,5},{2,6},{3,7},{4,8},{5,9},{6,10},{7,11},{8,12},{9,13},{1... | collective-permute-start | bytes 884744 | tf_op jit(solution)/shard_map/ppermute | solution.py:188
  26.9 6.0 %collective-permute-start.3 = (bf16[128,1152]{1,0:T(8,128)(2,1)S(1)}, bf16[128,1152]{1,0:T(8,128)(2,1)S(1)}, u32[]{:S(2)}, u32[]{:S(2)}) collective-permute-start(bf16[128,1152]{1,0:T(8,128)(2,1)S(1)} %shard_map.55.refs_0_), channel_id=1, source_target_pairs={{0,14},{1,15},{2,0},{3,1},{4,2},{5,3},{6,4},{7,5},{8,6},{9,7},{10,... | collective-permute-start | bytes 884744 | tf_op jit(solution)/shard_map/ppermute | solution.py:189
  33.0 1.9 %collective-permute-start.2 = (bf16[128,1152]{1,0:T(8,128)(2,1)S(1)}, bf16[128,1152]{1,0:T(8,128)(2,1)S(1)}, u32[]{:S(2)}, u32[]{:S(2)}) collective-permute-start(bf16[128,1152]{1,0:T(8,128)(2,1)S(1)} %shard_map.55.refs_0_), channel_id=1, source_target_pairs={{0,2},{1,3},{2,4},{3,5},{4,6},{5,7},{6,8},{7,9},{8,10},{9,11},{10,... | collective-permute-start | bytes 884744 | tf_op jit(solution)/shard_map/ppermute | solution.py:188
  34.9 3.2 %collective-permute-done.4.refs_4_ = bf16[128,1152]{1,0:T(8,128)(2,1)S(1)} collective-permute-done((bf16[128,1152]{1,0:T(8,128)(2,1)S(1)}, bf16[128,1152]{1,0:T(8,128)(2,1)S(1)}, u32[]{:S(2)}, u32[]{:S(2)}) %collective-permute-start.4) | collective-permute-done | bytes 294944 | tf_op jit(solution)/shard_map/ppermute | solution.py:189
  38.1 3.8 %collective-permute-start.5 = (bf16[128,1152]{1,0:T(8,128)(2,1)S(1)}, bf16[128,1152]{1,0:T(8,128)(2,1)S(1)}, u32[]{:S(2)}, u32[]{:S(2)}) collective-permute-start(bf16[128,1152]{1,0:T(8,128)(2,1)S(1)} %collective-permute-done.4.refs_4_), channel_id=1, source_target_pairs={{0,14},{1,15},{2,0},{3,1},{4,2},{5,3},{6,4},{7,5},{8,6},{9,7},{10,... | collective-permute-start | bytes 884744 | tf_op jit(solution)/shard_map/ppermute | solution.py:193
  41.9 2.9 %collective-permute-done.refs_3_ = bf16[128,1152]{1,0:T(8,128)(2,1)S(1)} collective-permute-done((bf16[128,1152]{1,0:T(8,128)(2,1)S(1)}, bf16[128,1152]{1,0:T(8,128)(2,1)S(1)}, u32[]{:S(2)}, u32[]{:S(2)}) %collective-permute-start) | collective-permute-done | bytes 294944 | tf_op jit(solution)/shard_map/ppermute | solution.py:188
  44.8 1.9 %collective-permute-start.1 = (bf16[128,1152]{1,0:T(8,128)(2,1)S(1)}, bf16[128,1152]{1,0:T(8,128)(2,1)S(1)}, u32[]{:S(2)}, u32[]{:S(2)}) collective-permute-start(bf16[128,1152]{1,0:T(8,128)(2,1)S(1)} %collective-permute-done.refs_3_), channel_id=1, source_target_pairs={{0,2},{1,3},{2,4},{3,5},{4,6},{5,7},{6,8},{7,9},{8,10},{9,11},{10,... | collective-permute-start | bytes 884744 | tf_op jit(solution)/shard_map/ppermute | solution.py:192
  46.8 1.9 %collective-permute-start.6 = (bf16[128,1152]{1,0:T(8,128)(2,1)S(1)}, bf16[128,1152]{1,0:T(8,128)(2,1)S(1)}, u32[]{:S(2)}, u32[]{:S(2)}) collective-permute-start(bf16[128,1152]{1,0:T(8,128)(2,1)S(1)} %broadcast_select_fusion), channel_id=1, source_target_pairs={{0,4},{1,13},{2,6},{3,15},{4,8},{5,1},{6,10},{7,3},{8,12},{9,5},{1... | collective-permute-start | bytes 884744 | tf_op jit(solution)/shard_map/ppermute | solution.py:196
  49.3 0.0 all-to-all-done.groups_ref
  49.3 2.9 %shard_map.57.recoupled_ref = bf16[192,2048]{1,0:T(8,128)(2,1)S(1)} custom-call(s32[1]{0:T(128)S(6)} %sub.7.live_ref, bf16[32,96,128]{2,1,0:T(8,128)(2,1)S(1)} %all-to-all-done.groups_ref, s32[1,2048]{1,0:T(1,128)S(1)} %get-tuple-element.11.order_ref, f32[1,2048]{1,0:T(1,128)S(1)} %get-tuple-element.12.weight_ref), custom_call_target="tpu_custom_call" | custom-call | tf_op jit(solution)/shard_map/pallas_call | solution.py:198
  52.2 3.7 %collective-permute-done.1.refs_5_ = bf16[128,1152]{1,0:T(8,128)(2,1)S(1)} collective-permute-done((bf16[128,1152]{1,0:T(8,128)(2,1)S(1)}, bf16[128,1152]{1,0:T(8,128)(2,1)S(1)}, u32[]{:S(2)}, u32[]{:S(2)}) %collective-permute-start.1) | collective-permute-done | bytes 294944 | tf_op jit(solution)/shard_map/ppermute | solution.py:192
  55.9 0.0 collective-permute-done.3.refs_2_
  55.9 0.0 collective-permute-done.2.refs_1_
  55.9 0.0 collective-permute-done.5.refs_6_
  55.9 6.3 %collective-permute-done.6.refs_7_ = bf16[128,1152]{1,0:T(8,128)(2,1)S(1)} collective-permute-done((bf16[128,1152]{1,0:T(8,128)(2,1)S(1)}, bf16[128,1152]{1,0:T(8,128)(2,1)S(1)}, u32[]{:S(2)}, u32[]{:S(2)}) %collective-permute-start.6) | collective-permute-done | bytes 294944 | tf_op jit(solution)/shard_map/ppermute | solution.py:196
  62.2 0.2 shard_map.58.own_ref
  62.4 1.9 %collective-permute-start.7 = (bf16[1024,1152]{1,0:T(8,128)(2,1)S(1)}, bf16[1024,1152]{1,0:T(8,128)(2,1)S(1)}, u32[]{:S(2)}, u32[]{:S(2)}) collective-permute-start(bf16[1024,1152]{1,0:T(8,128)(2,1)S(1)} %shard_map.58.own_ref), channel_id=1, source_target_pairs={{0,1},{1,0},{2,3},{3,2},{4,5},{5,4},{6,7},{7,6},{8,9},{9,8},{10,11... | collective-permute-start | bytes 7077896 | tf_op jit(solution)/shard_map/ppermute | solution.py:207
  64.3 4.5 %collective-permute-done.7.partner_ref = bf16[1024,1152]{1,0:T(8,128)(2,1)S(1)} collective-permute-done((bf16[1024,1152]{1,0:T(8,128)(2,1)S(1)}, bf16[1024,1152]{1,0:T(8,128)(2,1)S(1)}, u32[]{:S(2)}, u32[]{:S(2)}) %collective-permute-start.7) | collective-permute-done | bytes 2359328 | tf_op jit(solution)/shard_map/ppermute | solution.py:207
  68.8 4.9 %shard_map.59 = bf16[32,96,128]{2,1,0:T(8,128)(2,1)S(1)} custom-call(s32[1]{0:T(128)} %bitcast.core_ref, bf16[192,2048]{1,0:T(8,128)(2,1)S(1)} %shard_map.57.recoupled_ref, s32[1,2048]{1,0:T(1,128)S(1)} %get-tuple-element.11.order_ref, f32[1,2048]{1,0:T(1,128)S(1)} %get-tuple-element.12.weight_ref, bf16[1024,1152]{1,0:T(8,128)(2,1)S(1)} %shard_map.58.own_ref, ...), custom_call_target="tpu_custom_call" | custom-call | tf_op jit(solution)/shard_map/pallas_call | solution.py:208
  73.7 32.3 %all_to_all.10.groups_ref = bf16[32,96,128]{2,1,0:T(8,128)(2,1)S(1)} all-to-all(bf16[32,96,128]{2,1,0:T(8,128)(2,1)S(1)} %shard_map.59), channel_id=1, replica_groups=mesh['chan'=32,'row'=16] {'chan'}, dimensions={0} | all-to-all | bytes 1572864 | tf_op jit(solution)/shard_map/all_to_all | solution.py:219
  106.0 1.2 %shard_map.60 = bf16[192,2048]{1,0:T(8,128)(2,1)} custom-call(bf16[32,96,128]{2,1,0:T(8,128)(2,1)S(1)} %all_to_all.10.groups_ref), custom_call_target="tpu_custom_call" | custom-call | tf_op jit(solution)/shard_map/pallas_call | solution.py:220
  (1 shorter events, 0.0 us)
Async XLA Ops:
  0.0 1.1 %copy-start = (bf16[1,192,2048]{2,1,0:T(8,128)(2,1)S(1)}, bf16[1,192,2048]{2,1,0:T(8,128)(2,1)}, u32[]{:S(2)}) copy-start(bf16[1,192,2048]{2,1,0:T(8,128)(2,1)} %param.5) | copy-start | bytes 2359300
  1.1 0.7 copy-start.2
  1.8 0.7 copy-start.3
  2.5 11.4 %copy-start.1 = (bf16[1,128,2048]{2,1,0:T(8,128)(2,1)S(1)}, bf16[1,128,2048]{2,1,0:T(8,128)(2,1)}, u32[]{:S(2)}) copy-start(bf16[1,128,2048]{2,1,0:T(8,128)(2,1)} %param.6) | copy-start | bytes 1572868
  3.7 45.6 %all-to-all-start = ((bf16[32,96,128]{2,1,0:T(8,128)(2,1)}), bf16[32,96,128]{2,1,0:T(8,128)(2,1)S(1)}, u32[]{:S(2)}, u32[]{:S(2)}) async-start(bf16[32,96,128]{2,1,0:T(8,128)(2,1)} %get-tuple-element.10), calls=%async_computation | async-start | bytes 1572864 | tf_op jit(solution)/shard_map/all_to_all | solution.py:191
  14.1 24.0 %collective-permute-start.4 = (bf16[128,1152]{1,0:T(8,128)(2,1)S(1)}, bf16[128,1152]{1,0:T(8,128)(2,1)S(1)}, u32[]{:S(2)}, u32[]{:S(2)}) collective-permute-start(bf16[128,1152]{1,0:T(8,128)(2,1)S(1)} %shard_map.55.refs_0_), channel_id=1, source_target_pairs={{0,12},{1,13},{2,14},{3,15},{4,0},{5,1},{6,2},{7,3},{8,4},{9,5},{1... | collective-permute-start | bytes 884744 | tf_op jit(solution)/shard_map/ppermute | solution.py:189
  25.0 19.8 %collective-permute-start = (bf16[128,1152]{1,0:T(8,128)(2,1)S(1)}, bf16[128,1152]{1,0:T(8,128)(2,1)S(1)}, u32[]{:S(2)}, u32[]{:S(2)}) collective-permute-start(bf16[128,1152]{1,0:T(8,128)(2,1)S(1)} %shard_map.55.refs_0_), channel_id=1, source_target_pairs={{0,4},{1,5},{2,6},{3,7},{4,8},{5,9},{6,10},{7,11},{8,12},{9,13},{1... | collective-permute-start | bytes 884744 | tf_op jit(solution)/shard_map/ppermute | solution.py:188
  26.9 29.0 %collective-permute-start.3 = (bf16[128,1152]{1,0:T(8,128)(2,1)S(1)}, bf16[128,1152]{1,0:T(8,128)(2,1)S(1)}, u32[]{:S(2)}, u32[]{:S(2)}) collective-permute-start(bf16[128,1152]{1,0:T(8,128)(2,1)S(1)} %shard_map.55.refs_0_), channel_id=1, source_target_pairs={{0,14},{1,15},{2,0},{3,1},{4,2},{5,3},{6,4},{7,5},{8,6},{9,7},{10,... | collective-permute-start | bytes 884744 | tf_op jit(solution)/shard_map/ppermute | solution.py:189
  33.0 22.9 %collective-permute-start.2 = (bf16[128,1152]{1,0:T(8,128)(2,1)S(1)}, bf16[128,1152]{1,0:T(8,128)(2,1)S(1)}, u32[]{:S(2)}, u32[]{:S(2)}) collective-permute-start(bf16[128,1152]{1,0:T(8,128)(2,1)S(1)} %shard_map.55.refs_0_), channel_id=1, source_target_pairs={{0,2},{1,3},{2,4},{3,5},{4,6},{5,7},{6,8},{7,9},{8,10},{9,11},{10,... | collective-permute-start | bytes 884744 | tf_op jit(solution)/shard_map/ppermute | solution.py:188
  38.1 17.8 %collective-permute-start.5 = (bf16[128,1152]{1,0:T(8,128)(2,1)S(1)}, bf16[128,1152]{1,0:T(8,128)(2,1)S(1)}, u32[]{:S(2)}, u32[]{:S(2)}) collective-permute-start(bf16[128,1152]{1,0:T(8,128)(2,1)S(1)} %collective-permute-done.4.refs_4_), channel_id=1, source_target_pairs={{0,14},{1,15},{2,0},{3,1},{4,2},{5,3},{6,4},{7,5},{8,6},{9,7},{10,... | collective-permute-start | bytes 884744 | tf_op jit(solution)/shard_map/ppermute | solution.py:193
  44.8 11.1 %collective-permute-start.1 = (bf16[128,1152]{1,0:T(8,128)(2,1)S(1)}, bf16[128,1152]{1,0:T(8,128)(2,1)S(1)}, u32[]{:S(2)}, u32[]{:S(2)}) collective-permute-start(bf16[128,1152]{1,0:T(8,128)(2,1)S(1)} %collective-permute-done.refs_3_), channel_id=1, source_target_pairs={{0,2},{1,3},{2,4},{3,5},{4,6},{5,7},{6,8},{7,9},{8,10},{9,11},{10,... | collective-permute-start | bytes 884744 | tf_op jit(solution)/shard_map/ppermute | solution.py:192
  46.8 15.4 %collective-permute-start.6 = (bf16[128,1152]{1,0:T(8,128)(2,1)S(1)}, bf16[128,1152]{1,0:T(8,128)(2,1)S(1)}, u32[]{:S(2)}, u32[]{:S(2)}) collective-permute-start(bf16[128,1152]{1,0:T(8,128)(2,1)S(1)} %broadcast_select_fusion), channel_id=1, source_target_pairs={{0,4},{1,13},{2,6},{3,15},{4,8},{5,1},{6,10},{7,3},{8,12},{9,5},{1... | collective-permute-start | bytes 884744 | tf_op jit(solution)/shard_map/ppermute | solution.py:196
  62.4 6.4 %collective-permute-start.7 = (bf16[1024,1152]{1,0:T(8,128)(2,1)S(1)}, bf16[1024,1152]{1,0:T(8,128)(2,1)S(1)}, u32[]{:S(2)}, u32[]{:S(2)}) collective-permute-start(bf16[1024,1152]{1,0:T(8,128)(2,1)S(1)} %shard_map.58.own_ref), channel_id=1, source_target_pairs={{0,1},{1,0},{2,3},{3,2},{4,5},{5,4},{6,7},{7,6},{8,9},{9,8},{10,11... | collective-permute-start | bytes 7077896 | tf_op jit(solution)/shard_map/ppermute | solution.py:207

commit v4 on v3

--- a/solution.py
+++ b/solution.py
@@ -71,7 +71,19 @@
     return jnp.where(rows == order, 1.0, 0.0).astype(jnp.bfloat16)
 
 
-def recouple_body(live_ref, groups_ref, order_ref, weight_ref, out_ref, gathered):
+def rotated(table_ref, first, out_ref):
+    blocks = out_ref.shape[1] // BLOCK
+    for step in range(blocks):
+        at = pl.multiple_of((first + step) % blocks * BLOCK, BLOCK)
+        out_ref[:, step * BLOCK : (step + 1) * BLOCK] = table_ref[:, pl.ds(at, BLOCK)]
+
+
+def recouple_body(
+    live_ref, row_ref, groups_ref, order_in, weight_in, out_ref, order_ref, weight_ref, gathered
+):
+    first = row_ref[0] - row_ref[0] % 2
+    rotated(order_in, first, order_ref)
+    rotated(weight_in, first, weight_ref)
     unpack_body(groups_ref, gathered)
     row_count, col_count = out_ref.shape
     live = lax.broadcasted_iota(jnp.int32, (row_count, TILE), 0) < live_ref[0]
@@ -84,13 +96,6 @@
         out_ref[:, at : at + TILE] = jnp.where(live, taken, 0.0).astype(out_ref.dtype)
 
 
-def rotated(table_ref, first, out_ref):
-    blocks = out_ref.shape[1] // BLOCK
-    for step in range(blocks):
-        at = pl.multiple_of((first + step) % blocks * BLOCK, BLOCK)
-        out_ref[:, step * BLOCK : (step + 1) * BLOCK] = table_ref[:, pl.ds(at, BLOCK)]
-
-
 def halve_body(row_ref, panel_ref, out_ref):
     blocks = panel_ref.shape[1] // BLOCK
     for step in range(out_ref.shape[1] // BLOCK):
@@ -98,27 +103,41 @@
         out_ref[:, step * BLOCK : (step + 1) * BLOCK] = panel_ref[:, pl.ds(at, BLOCK)]
 
 
-def send_body(row_ref, block_ref, order_ref, weight_ref, out_ref, order_out, weight_out):
-    pack_body(block_ref, out_ref)
-    first = row_ref[0] - row_ref[0] % 2
-    rotated(order_ref, first, order_out)
-    rotated(weight_ref, first, weight_out)
-
-
 def stack_body(*refs):
     pieces, out_ref = refs[:-1], refs[-1]
     for number, piece in enumerate(pieces):
         out_ref[number * BLOCK : (number + 1) * BLOCK] = piece[...]
 
 
-def product_body(core_ref, recoupled_ref, order_ref, weight_ref, own_ref, partner_ref, *refs):
+def product_body(core_ref, recoupled_ref, order_ref, weight_ref, *refs):
     row_count, col_count = recoupled_ref.shape
     blocks = col_count // BLOCK
-    out_ref, panel, scaled, restored = refs
-    width = own_ref.shape[1]
-
-    def place(stack, parity):
-        for number, chip in enumerate(CHIPS):
+    own_near, partner_near, own_far, partner_far, out_ref, panel, scaled, restored, sems = refs
+    width = own_near.shape[1]
+
+    def bring(stack, chips, parity):
+        copies = []
+        for number, chip in enumerate(chips):
+            first = (2 * (chip % (blocks // 2)) + parity) * BLOCK
+            inside = min(width, col_count - first)
+            source, target = pl.ds(number * BLOCK, BLOCK), pl.ds(first, BLOCK)
+            parts = [(0, first, inside)]
+            if inside < width:
+                parts.append((inside, 0, width - inside))
+            for left, column, size in parts:
+                copies.append(
+                    pltpu.make_async_copy(
+                        stack.at[source, pl.ds(left, size)],
+                        panel.at[target, pl.ds(column, size)],
+                        sems.at[len(copies)],
+                    )
+                )
+        for copy in copies:
+            copy.start()
+        return copies
+
+    def place(stack, chips, parity):
+        for number, chip in enumerate(chips):
             first = (2 * (chip % (blocks // 2)) + parity) * BLOCK
             inside = min(width, col_count - first)
             source = slice(number * BLOCK, (number + 1) * BLOCK)
@@ -130,8 +149,12 @@
 
         @pl.when(core_ref[0] == parity)
         def _(parity=parity):
-            place(own_ref, parity)
-            place(partner_ref, 1 - parity)
+            copies = bring(partner_near, CHIPS[:NEAR], 1 - parity)
+            place(own_near, CHIPS[:NEAR], parity)
+            place(own_far, CHIPS[NEAR:], parity)
+            place(partner_far, CHIPS[NEAR:], 1 - parity)
+            for copy in copies:
+                copy.wait()
 
     for block in range(blocks):
         own = slice(block * BLOCK, (block + 1) * BLOCK)
@@ -153,6 +176,7 @@
     pack_body(restored, out_ref)
 
 
+NEAR = 5
 CHIPS = (0, -1, 1, -2, 2, -3, 3, 4)
 
 
@@ -176,45 +200,50 @@
         return [(row, (row + 2 * far) % rows) for row in range(rows)]
 
     swap = [(row, row ^ 1) for row in range(rows)]
-    sent, order, weight = call(
-        send_body,
+    sent = call(pack_body, packed, [vmem()])(own_block)
+    from_below, from_above = [own_half], [own_half]
+    for _ in range(3):
+        from_below.append(lax.ppermute(from_below[-1], "row", hop(1)))
+        from_above.append(lax.ppermute(from_above[-1], "row", hop(-1)))
+    sent = near_core(sent)
+    groups = lax.all_to_all(sent, "chan", split_axis=0, concat_axis=0, tiled=True)
+    apart = list(zip(hop(1), hop(-1)))
+    passed = jnp.where(core == 0, from_below[3], from_above[3])
+    opposite = lax.ppermute(passed, "row", [pair[row % 2] for row, pair in enumerate(apart)])
+    live_rows = row_counts - row_at * row_count
+    recoupled, order, weight = call(
+        recouple_body,
         (
-            packed,
+            flat,
             jax.ShapeDtypeStruct(column_order.shape, column_order.dtype),
             jax.ShapeDtypeStruct(weights6j.shape, weights6j.dtype),
         ),
-        [smem(), vmem(), vmem(), vmem()],
-    )(row_at[None], own_block, column_order, weights6j)
-    from_below = [lax.ppermute(own_half, "row", hop(far)) for far in (1, 2)]
-    from_above = [lax.ppermute(own_half, "row", hop(-far)) for far in (1, 2)]
-    sent = near_core(sent)
-    groups = lax.all_to_all(sent, "chan", split_axis=0, concat_axis=0, tiled=True)
-    third_below = lax.ppermute(from_below[1], "row", hop(1))
-    third_above = lax.ppermute(from_above[1], "row", hop(-1))
-    apart = list(zip(hop(2), hop(-2)))
-    passed = jnp.where(core == 0, from_below[1], from_above[1])
-    opposite = lax.ppermute(passed, "row", [pair[row % 2] for row, pair in enumerate(apart)])
-    live_rows = row_counts - row_at * row_count
-    recoupled = call(
-        recouple_body, flat, [smem(), vmem(), vmem(), vmem()], [pltpu.VMEM(flat.shape, dtype)]
-    )(live_rows, near_core(groups), order, weight)
-    third_below, recoupled = lax.optimization_barrier((third_below, recoupled))
-    pieces = [own_half, from_below[0], from_above[0], from_below[1], from_above[1]]
-    pieces += [third_below, third_above, opposite]
-    stack_shape = jax.ShapeDtypeStruct((len(pieces) * BLOCK, half.shape[1]), dtype)
-    stack = call(stack_body, stack_shape, [vmem()] * len(pieces))(*map(near_core, pieces))
-    stack = near_core(stack)
-    partner = near_core(lax.ppermute(stack, "row", swap))
+        [smem(), smem(), *[vmem()] * 3],
+        [pltpu.VMEM(flat.shape, dtype)],
+    )(live_rows, row_at[None], near_core(groups), column_order, weights6j)
+    from_below[3], recoupled = lax.optimization_barrier((from_below[3], recoupled))
+    pieces = [own_half]
+    for pair in zip(from_below[1:], from_above[1:]):
+        pieces += pair
+    pieces.append(opposite)
+    def stacked(some):
+        shape = jax.ShapeDtypeStruct((len(some) * BLOCK, half.shape[1]), dtype)
+        stack = near_core(call(stack_body, shape, [vmem()] * len(some))(*map(near_core, some)))
+        return [stack, lax.ppermute(stack, "row", swap)]
+
+    stacks = [*stacked(pieces[:NEAR]), *stacked(pieces[NEAR:])]
+    stacks[3] = near_core(stacks[3])
     restored = call(
         product_body,
         packed,
-        [smem(), *[vmem()] * 5],
+        [smem(), *[vmem()] * 4, anywhere(), *[vmem()] * 2],
         [
             pltpu.VMEM((col_count, col_count), dtype),
             pltpu.VMEM(flat.shape, dtype),
             pltpu.VMEM(flat.shape, dtype),
+            pltpu.SemaphoreType.DMA((2 * NEAR,)),
         ],
-    )(core[None], near_core(recoupled), order, weight, stack, partner)
+    )(core[None], near_core(recoupled), order, weight, *stacks)
     restored = near_core(restored)
     returned = lax.all_to_all(restored, "chan", split_axis=0, concat_axis=0, tiled=True)
     return call(unpack_body, flat, [vmem()])(near_core(returned))[None]

time: 108 us -> 107 us (level)
  waiting for transfers between devices: 20.5 us -> 13.3 us
  starting transfers between devices: 40.6 us -> 43.5 us
  Pallas kernels: 10.4 us -> 12.6 us
  local copies, waits for them, and re-layouts: 2.53 us -> 3.83 us
    ppermute x7 -> x8, waiting for transfers between devices: 14.2 us -> 8.87 us  [the longest x3 4.01 us: per_device(): from_below.append(lax.ppermute(from_below[-1], 'row', hop(1)))]
    ppermute x7 -> x8, starting transfers between devices: 28.4 us -> 31.4 us  [the longest x3 21.8 us: per_device(): from_above.append(lax.ppermute(from_above[-1], 'row', hop(-1)))]
    pallas_call x4 -> x5, Pallas kernels: 9.12 us -> 11.3 us  [the longest x1 6.01 us: per_device(): call(product_body, packed, [smem(), *[vmem()] * 4, anywhere(), *[vmem()]...]
    ppermute x1, waiting for transfers between devices: 6.3 us -> 4.38 us  [per_device(): lax.ppermute(passed, 'row', [pair[row % 2] for row, pair in enumerate(apa...]
    unnamed x8 -> x12, local copies, waits for them, and re-layouts: 2.53 us -> 3.83 us
  transfers between devices with their start and end apart: 9 -> 10, of which waited for: 5 -> 4; matrix products, arithmetic and copies ran while one was open for 0% -> 0% of each run, Pallas kernels for 3% -> 5%
where the time goes in v4:
time: 107 us; the launch traced here: 106 us
  starting transfers between devices  43.5 us (41%)
  blocking collectives  32.4 us (30%)
  waiting for transfers between devices  13.3 us (12%)
  Pallas kernels  12.6 us (12%)
  local copies, waits for them, and re-layouts  3.83 us (4%)
    all_to_all x1, blocking collectives, per_device(): lax.all_to_all(restored, 'chan', split_axis=0, concat_axis=0, tiled=True)  32.4 us
    ppermute x3, starting transfers between devices, per_device(): from_above.append(lax.ppermute(from_above[-1], 'row', hop(-1)))  21.8 us
    all_to_all x1, starting transfers between devices, per_device(): lax.all_to_all(sent, 'chan', split_axis=0, concat_axis=0, tiled=True)  10.2 us
    pallas_call x1, Pallas kernels, per_device(): call(product_body, packed, [smem(), *[vmem()] * 4, anywhere(), *[vmem()]...  6.01 us
    ppermute x3, starting transfers between devices, per_device(): from_below.append(lax.ppermute(from_below[-1], 'row', hop(1)))  5.76 us
    ppermute x1, waiting for transfers between devices, per_device(): lax.ppermute(passed, 'row', [pair[row % 2] for row, pair in enumerate(apa...  4.38 us
    ppermute x3, waiting for transfers between devices, per_device(): from_below.append(lax.ppermute(from_below[-1], 'row', hop(1)))  4.01 us
    ppermute x2, starting transfers between devices, stacked(): return [stack, lax.ppermute(stack, 'row', swap)]  3.84 us
  transfers between devices with their start and end apart: 10, of which 4 were waited for; matrix products, arithmetic and copies ran while one was open for 0% of the time, Pallas kernels for 5%

profile of v4, /device:TPU:6, one launch (start us, length us, event | category | flops | bytes accessed | tf_op | source)
XLA Modules:
  0.0 106.5 jit_solution(7375339290889492113)
XLA Ops:
  0.0 0.0 copy-start.1
  0.0 1.0 copy-done.1
  1.0 0.1 shard_map.55.refs_0_
  1.1 10.9 %collective-permute-start.3 = (bf16[128,1152]{1,0:T(8,128)(2,1)S(1)}, bf16[128,1152]{1,0:T(8,128)(2,1)S(1)}, u32[]{:S(2)}, u32[]{:S(2)}) collective-permute-start(bf16[128,1152]{1,0:T(8,128)(2,1)S(1)} %shard_map.55.refs_0_), channel_id=1, source_target_pairs={{0,14},{1,15},{2,0},{3,1},{4,2},{5,3},{6,4},{7,5},{8,6},{9,7},{10,... | collective-permute-start | bytes 884744 | tf_op jit(solution)/shard_map/ppermute | solution.py:207
  12.1 1.9 %collective-permute-start = (bf16[128,1152]{1,0:T(8,128)(2,1)S(1)}, bf16[128,1152]{1,0:T(8,128)(2,1)S(1)}, u32[]{:S(2)}, u32[]{:S(2)}) collective-permute-start(bf16[128,1152]{1,0:T(8,128)(2,1)S(1)} %shard_map.55.refs_0_), channel_id=1, source_target_pairs={{0,2},{1,3},{2,4},{3,5},{4,6},{5,7},{6,8},{7,9},{8,10},{9,11},{10,... | collective-permute-start | bytes 884744 | tf_op jit(solution)/shard_map/ppermute | solution.py:206
  14.0 0.0 copy-start
  14.0 1.1 %copy-done = bf16[1,192,2048]{2,1,0:T(8,128)(2,1)S(1)} copy-done((bf16[1,192,2048]{2,1,0:T(8,128)(2,1)S(1)}, bf16[1,192,2048]{2,1,0:T(8,128)(2,1)}, u32[]{:S(2)}) %copy-start) | copy-done | bytes 786456
  15.1 1.2 %shard_map.56 = bf16[32,96,128]{2,1,0:T(8,128)(2,1)} custom-call(bf16[192,2048]{1,0:T(8,128)(2,1)S(1)} %bitcast.6), custom_call_target="tpu_custom_call" | custom-call | tf_op jit(solution)/shard_map/pallas_call | solution.py:203
  16.3 10.2 %all-to-all-start = ((bf16[32,96,128]{2,1,0:T(8,128)(2,1)}), bf16[32,96,128]{2,1,0:T(8,128)(2,1)S(1)}, u32[]{:S(2)}, u32[]{:S(2)}) async-start(bf16[32,96,128]{2,1,0:T(8,128)(2,1)} %shard_map.56), calls=%async_computation | async-start | bytes 1572864 | tf_op jit(solution)/shard_map/all_to_all | solution.py:209
  26.6 0.0 collective-permute-done.3.refs_2_
  26.6 5.1 %collective-permute-start.4 = (bf16[128,1152]{1,0:T(8,128)(2,1)S(1)}, bf16[128,1152]{1,0:T(8,128)(2,1)}, u32[]{:S(2)}, u32[]{:S(2)}) collective-permute-start(bf16[128,1152]{1,0:T(8,128)(2,1)S(1)} %collective-permute-done.3.refs_2_), channel_id=1, source_target_pairs={{0,14},{1,15},{2,0},{3,1},{4,2},{5,3},{6,4},{7,5},{8,6},{9,7},{10,... | collective-permute-start | bytes 884744 | tf_op jit(solution)/shard_map/ppermute | solution.py:207
  31.7 0.0 collective-permute-done.refs_1_
  31.7 1.9 %collective-permute-start.1 = (bf16[128,1152]{1,0:T(8,128)(2,1)S(1)}, bf16[128,1152]{1,0:T(8,128)(2,1)}, u32[]{:S(2)}, u32[]{:S(2)}) collective-permute-start(bf16[128,1152]{1,0:T(8,128)(2,1)S(1)} %collective-permute-done.refs_1_), channel_id=1, source_target_pairs={{0,2},{1,3},{2,4},{3,5},{4,6},{5,7},{6,8},{7,9},{8,10},{9,11},{10,... | collective-permute-start | bytes 884744 | tf_op jit(solution)/shard_map/ppermute | solution.py:206
  33.6 0.0 copy-start.2
  33.7 0.7 copy-done.2
  34.4 2.5 %collective-permute-done.4.refs_4_ = bf16[128,1152]{1,0:T(8,128)(2,1)} collective-permute-done((bf16[128,1152]{1,0:T(8,128)(2,1)S(1)}, bf16[128,1152]{1,0:T(8,128)(2,1)}, u32[]{:S(2)}, u32[]{:S(2)}) %collective-permute-start.4) | collective-permute-done | bytes 294944 | tf_op jit(solution)/shard_map/ppermute | solution.py:207
  36.8 5.7 %collective-permute-start.6 = (bf16[128,1152]{1,0:T(8,128)(2,1)}, bf16[128,1152]{1,0:T(8,128)(2,1)S(1)}, u32[]{:S(2)}, u32[]{:S(2)}) collective-permute-start(bf16[128,1152]{1,0:T(8,128)(2,1)} %collective-permute-done.4.refs_4_), channel_id=1, source_target_pairs={{0,14},{1,15},{2,0},{3,1},{4,2},{5,3},{6,4},{7,5},{8,6},{9,7},{10,... | collective-permute-start | bytes 884744 | tf_op jit(solution)/shard_map/ppermute | solution.py:207
  42.5 0.0 collective-permute-done.1.refs_3_
  42.5 1.9 %collective-permute-start.2 = (bf16[128,1152]{1,0:T(8,128)(2,1)}, bf16[128,1152]{1,0:T(8,128)(2,1)S(1)}, u32[]{:S(2)}, u32[]{:S(2)}) collective-permute-start(bf16[128,1152]{1,0:T(8,128)(2,1)} %collective-permute-done.1.refs_3_), channel_id=1, source_target_pairs={{0,2},{1,3},{2,4},{3,5},{4,6},{5,7},{6,8},{7,9},{8,10},{9,11},{10,... | collective-permute-start | bytes 884744 | tf_op jit(solution)/shard_map/ppermute | solution.py:206
  44.5 0.0 copy-start.3
  44.5 1.0 copy-done.3
  45.4 0.0 copy-start.4
  45.4 0.0 copy-start.5
  45.4 1.2 %shard_map.58.refs_0_ = bf16[640,1152]{1,0:T(8,128)(2,1)S(1)} custom-call(bf16[128,1152]{1,0:T(8,128)(2,1)S(1)} %shard_map.55.refs_0_, bf16[128,1152]{1,0:T(8,128)(2,1)S(1)} %copy-done.3, bf16[128,1152]{1,0:T(8,128)(2,1)S(1)} %collective-permute-done.3.refs_2_, bf16[128,1152]{1,0:T(8,128)(2,1)} %collective-permute-done.1.refs_3_, ...), custom_call_target="tpu_custom_call" | custom-call | tf_op jit(solution)/shard_map/pallas_call | solution.py:231
  46.6 1.9 %collective-permute-start.5 = (bf16[640,1152]{1,0:T(8,128)(2,1)S(1)}, bf16[640,1152]{1,0:T(8,128)(2,1)}, u32[]{:S(2)}, u32[]{:S(2)}) collective-permute-start(bf16[640,1152]{1,0:T(8,128)(2,1)S(1)} %shard_map.58.refs_0_), channel_id=1, source_target_pairs={{0,1},{1,0},{2,3},{3,2},{4,5},{5,4},{6,7},{7,6},{8,9},{9,8},{10,11... | collective-permute-start | bytes 4423688 | tf_op jit(solution)/shard_map/ppermute | solution.py:232
  48.6 0.0 collective-permute-done.6.refs_1_
  48.6 4.0 %collective-permute-done.2.refs_0_ = bf16[128,1152]{1,0:T(8,128)(2,1)S(1)} collective-permute-done((bf16[128,1152]{1,0:T(8,128)(2,1)}, bf16[128,1152]{1,0:T(8,128)(2,1)S(1)}, u32[]{:S(2)}, u32[]{:S(2)}) %collective-permute-start.2) | collective-permute-done | bytes 294944 | tf_op jit(solution)/shard_map/ppermute | solution.py:206
  52.6 1.9 %collective-permute-start.7 = (bf16[128,1152]{1,0:T(8,128)(2,1)S(1)}, bf16[128,1152]{1,0:T(8,128)(2,1)S(1)}, u32[]{:S(2)}, u32[]{:S(2)}) collective-permute-start(bf16[128,1152]{1,0:T(8,128)(2,1)S(1)} %broadcast_select_fusion), channel_id=1, source_target_pairs={{0,2},{1,15},{2,4},{3,1},{4,6},{5,3},{6,8},{7,5},{8,10},{9,7},{10,... | collective-permute-start | bytes 884744 | tf_op jit(solution)/shard_map/ppermute | solution.py:212
  55.2 0.0 all-to-all-done.groups_ref
  55.2 0.0 copy-done.4
  55.2 0.0 copy-done.5
  55.2 2.8 %shard_map.57 = (bf16[192,2048]{1,0:T(8,128)(2,1)S(1)}, s32[1,2048]{1,0:T(1,128)S(1)}, f32[1,2048]{1,0:T(1,128)S(1)}) custom-call(s32[1]{0:T(128)S(6)} %sub.7.live_ref, s32[1]{0:T(128)} %bitcast.1.row_ref, bf16[32,96,128]{2,1,0:T(8,128)(2,1)S(1)} %all-to-all-done.groups_ref, s32[1,2048]{1,0:T(1,128)S(1)} %copy-done.4, f32[1,2048]{1,0:T(1,128)S(1)} %copy-done.5), custom_call_target="tpu_custom_call" | custom-call | tf_op jit(solution)/shard_map/pallas_call | solution.py:214
  58.1 4.4 %collective-permute-done.7.refs_2_ = bf16[128,1152]{1,0:T(8,128)(2,1)S(1)} collective-permute-done((bf16[128,1152]{1,0:T(8,128)(2,1)S(1)}, bf16[128,1152]{1,0:T(8,128)(2,1)S(1)}, u32[]{:S(2)}, u32[]{:S(2)}) %collective-permute-start.7) | collective-permute-done | bytes 294944 | tf_op jit(solution)/shard_map/ppermute | solution.py:212
  62.4 0.1 shard_map.59.refs_2_
  62.5 1.9 %collective-permute-start.8 = (bf16[384,1152]{1,0:T(8,128)(2,1)S(1)}, bf16[384,1152]{1,0:T(8,128)(2,1)S(1)}, u32[]{:S(2)}, u32[]{:S(2)}) collective-permute-start(bf16[384,1152]{1,0:T(8,128)(2,1)S(1)} %shard_map.59.refs_2_), channel_id=1, source_target_pairs={{0,1},{1,0},{2,3},{3,2},{4,5},{5,4},{6,7},{7,6},{8,9},{9,8},{10,11... | collective-permute-start | bytes 2654216 | tf_op jit(solution)/shard_map/ppermute | solution.py:232
  64.4 0.0 collective-permute-done.5.refs_1_
  64.5 2.4 %collective-permute-done.8.refs_3_ = bf16[384,1152]{1,0:T(8,128)(2,1)S(1)} collective-permute-done((bf16[384,1152]{1,0:T(8,128)(2,1)S(1)}, bf16[384,1152]{1,0:T(8,128)(2,1)S(1)}, u32[]{:S(2)}, u32[]{:S(2)}) %collective-permute-start.8) | collective-permute-done | bytes 884768 | tf_op jit(solution)/shard_map/ppermute | solution.py:232
  66.8 6.0 %shard_map.60 = bf16[32,96,128]{2,1,0:T(8,128)(2,1)S(1)} custom-call(s32[1]{0:T(128)} %bitcast.core_ref, bf16[192,2048]{1,0:T(8,128)(2,1)S(1)} %get-tuple-element.11.recoupled_ref, s32[1,2048]{1,0:T(1,128)S(1)} %get-tuple-element.12.order_ref, f32[1,2048]{1,0:T(1,128)S(1)} %get-tuple-element.13.weight_ref, bf16[640,1152]{1,0:T(8,128)(2,1)S(1)} %shard_map.58.refs_0_, ...), custom_call_target="tpu_custom_call" | custom-call | tf_op jit(solution)/shard_map/pallas_call | solution.py:236
  72.9 32.4 %all_to_all.10.groups_ref = bf16[32,96,128]{2,1,0:T(8,128)(2,1)S(1)} all-to-all(bf16[32,96,128]{2,1,0:T(8,128)(2,1)S(1)} %shard_map.60), channel_id=1, replica_groups=mesh['chan'=32,'row'=16] {'chan'}, dimensions={0} | all-to-all | bytes 1572864 | tf_op jit(solution)/shard_map/all_to_all | solution.py:248
  105.2 1.2 %shard_map.61 = bf16[192,2048]{1,0:T(8,128)(2,1)} custom-call(bf16[32,96,128]{2,1,0:T(8,128)(2,1)S(1)} %all_to_all.10.groups_ref), custom_call_target="tpu_custom_call" | custom-call | tf_op jit(solution)/shard_map/pallas_call | solution.py:249
  (1 shorter events, 0.0 us)
Async XLA Ops:
  0.0 1.0 copy-start.1
  1.1 25.4 %collective-permute-start.3 = (bf16[128,1152]{1,0:T(8,128)(2,1)S(1)}, bf16[128,1152]{1,0:T(8,128)(2,1)S(1)}, u32[]{:S(2)}, u32[]{:S(2)}) collective-permute-start(bf16[128,1152]{1,0:T(8,128)(2,1)S(1)} %shard_map.55.refs_0_), channel_id=1, source_target_pairs={{0,14},{1,15},{2,0},{3,1},{4,2},{5,3},{6,4},{7,5},{8,6},{9,7},{10,... | collective-permute-start | bytes 884744 | tf_op jit(solution)/shard_map/ppermute | solution.py:207
  12.1 19.6 %collective-permute-start = (bf16[128,1152]{1,0:T(8,128)(2,1)S(1)}, bf16[128,1152]{1,0:T(8,128)(2,1)S(1)}, u32[]{:S(2)}, u32[]{:S(2)}) collective-permute-start(bf16[128,1152]{1,0:T(8,128)(2,1)S(1)} %shard_map.55.refs_0_), channel_id=1, source_target_pairs={{0,2},{1,3},{2,4},{3,5},{4,6},{5,7},{6,8},{7,9},{8,10},{9,11},{10,... | collective-permute-start | bytes 884744 | tf_op jit(solution)/shard_map/ppermute | solution.py:206
  14.0 1.1 %copy-start = (bf16[1,192,2048]{2,1,0:T(8,128)(2,1)S(1)}, bf16[1,192,2048]{2,1,0:T(8,128)(2,1)}, u32[]{:S(2)}) copy-start(bf16[1,192,2048]{2,1,0:T(8,128)(2,1)} %param.5) | copy-start | bytes 2359300
  16.3 38.8 %all-to-all-start = ((bf16[32,96,128]{2,1,0:T(8,128)(2,1)}), bf16[32,96,128]{2,1,0:T(8,128)(2,1)S(1)}, u32[]{:S(2)}, u32[]{:S(2)}) async-start(bf16[32,96,128]{2,1,0:T(8,128)(2,1)} %shard_map.56), calls=%async_computation | async-start | bytes 1572864 | tf_op jit(solution)/shard_map/all_to_all | solution.py:209
  26.6 10.3 %collective-permute-start.4 = (bf16[128,1152]{1,0:T(8,128)(2,1)S(1)}, bf16[128,1152]{1,0:T(8,128)(2,1)}, u32[]{:S(2)}, u32[]{:S(2)}) collective-permute-start(bf16[128,1152]{1,0:T(8,128)(2,1)S(1)} %collective-permute-done.3.refs_2_), channel_id=1, source_target_pairs={{0,14},{1,15},{2,0},{3,1},{4,2},{5,3},{6,4},{7,5},{8,6},{9,7},{10,... | collective-permute-start | bytes 884744 | tf_op jit(solution)/shard_map/ppermute | solution.py:207
  31.7 10.8 %collective-permute-start.1 = (bf16[128,1152]{1,0:T(8,128)(2,1)S(1)}, bf16[128,1152]{1,0:T(8,128)(2,1)}, u32[]{:S(2)}, u32[]{:S(2)}) collective-permute-start(bf16[128,1152]{1,0:T(8,128)(2,1)S(1)} %collective-permute-done.refs_1_), channel_id=1, source_target_pairs={{0,2},{1,3},{2,4},{3,5},{4,6},{5,7},{6,8},{7,9},{8,10},{9,11},{10,... | collective-permute-start | bytes 884744 | tf_op jit(solution)/shard_map/ppermute | solution.py:206
  33.6 0.7 copy-start.2
  36.8 11.7 %collective-permute-start.6 = (bf16[128,1152]{1,0:T(8,128)(2,1)}, bf16[128,1152]{1,0:T(8,128)(2,1)S(1)}, u32[]{:S(2)}, u32[]{:S(2)}) collective-permute-start(bf16[128,1152]{1,0:T(8,128)(2,1)} %collective-permute-done.4.refs_4_), channel_id=1, source_target_pairs={{0,14},{1,15},{2,0},{3,1},{4,2},{5,3},{6,4},{7,5},{8,6},{9,7},{10,... | collective-permute-start | bytes 884744 | tf_op jit(solution)/shard_map/ppermute | solution.py:207
  42.5 10.0 %collective-permute-start.2 = (bf16[128,1152]{1,0:T(8,128)(2,1)}, bf16[128,1152]{1,0:T(8,128)(2,1)S(1)}, u32[]{:S(2)}, u32[]{:S(2)}) collective-permute-start(bf16[128,1152]{1,0:T(8,128)(2,1)} %collective-permute-done.1.refs_3_), channel_id=1, source_target_pairs={{0,2},{1,3},{2,4},{3,5},{4,6},{5,7},{6,8},{7,9},{8,10},{9,11},{10,... | collective-permute-start | bytes 884744 | tf_op jit(solution)/shard_map/ppermute | solution.py:206
  44.5 1.0 copy-start.3
  45.4 9.8 %copy-start.4 = (s32[1,2048]{1,0:T(1,128)S(1)}, s32[1,2048]{1,0:T(1,128)}, u32[]{:S(2)}) copy-start(s32[1,2048]{1,0:T(1,128)} %order_in.1) | copy-start | bytes 24580
  45.4 9.8 %copy-start.5 = (f32[1,2048]{1,0:T(1,128)S(1)}, f32[1,2048]{1,0:T(1,128)}, u32[]{:S(2)}) copy-start(f32[1,2048]{1,0:T(1,128)} %weight_in.1) | copy-start | bytes 24580
  46.6 17.8 %collective-permute-start.5 = (bf16[640,1152]{1,0:T(8,128)(2,1)S(1)}, bf16[640,1152]{1,0:T(8,128)(2,1)}, u32[]{:S(2)}, u32[]{:S(2)}) collective-permute-start(bf16[640,1152]{1,0:T(8,128)(2,1)S(1)} %shard_map.58.refs_0_), channel_id=1, source_target_pairs={{0,1},{1,0},{2,3},{3,2},{4,5},{5,4},{6,7},{7,6},{8,9},{9,8},{10,11... | collective-permute-start | bytes 4423688 | tf_op jit(solution)/shard_map/ppermute | solution.py:232
  52.6 9.8 %collective-permute-start.7 = (bf16[128,1152]{1,0:T(8,128)(2,1)S(1)}, bf16[128,1152]{1,0:T(8,128)(2,1)S(1)}, u32[]{:S(2)}, u32[]{:S(2)}) collective-permute-start(bf16[128,1152]{1,0:T(8,128)(2,1)S(1)} %broadcast_select_fusion), channel_id=1, source_target_pairs={{0,2},{1,15},{2,4},{3,1},{4,6},{5,3},{6,8},{7,5},{8,10},{9,7},{10,... | collective-permute-start | bytes 884744 | tf_op jit(solution)/shard_map/ppermute | solution.py:212
  62.5 4.3 %collective-permute-start.8 = (bf16[384,1152]{1,0:T(8,128)(2,1)S(1)}, bf16[384,1152]{1,0:T(8,128)(2,1)S(1)}, u32[]{:S(2)}, u32[]{:S(2)}) collective-permute-start(bf16[384,1152]{1,0:T(8,128)(2,1)S(1)} %shard_map.59.refs_2_), channel_id=1, source_target_pairs={{0,1},{1,0},{2,3},{3,2},{4,5},{5,4},{6,7},{7,6},{8,9},{9,8},{10,11... | collective-permute-start | bytes 2654216 | tf_op jit(solution)/shard_map/ppermute | solution.py:232

commit v5 on v4

--- a/solution.py
+++ b/solution.py
@@ -176,7 +176,7 @@
     pack_body(restored, out_ref)
 
 
-NEAR = 5
+NEAR = 4
 CHIPS = (0, -1, 1, -2, 2, -3, 3, 4)
 
 

time: 107 us -> 108 us (level)
    ppermute x1, waiting for transfers between devices: 4.38 us -> 0.72 us  [per_device(): lax.ppermute(passed, 'row', [pair[row % 2] for row, pair in enumerate(apa...]
    ppermute x3, waiting for transfers between devices: 2.48 us -> 4.74 us  [per_device(): from_above.append(lax.ppermute(from_above[-1], 'row', hop(-1)))]
    ppermute x3, waiting for transfers between devices: 4.01 us -> 5.63 us  [per_device(): from_below.append(lax.ppermute(from_below[-1], 'row', hop(1)))]
    unnamed x12 -> x16, local copies, waits for them, and re-layouts: 3.83 us -> 3.75 us
  transfers between devices with their start and end apart: 10 -> 10, of which waited for: 4 -> 5; matrix products, arithmetic and copies ran while one was open for 0% -> 1% of each run, Pallas kernels for 5% -> 5%
where the time goes in v5:
time: 108 us; the launch traced here: 107 us
  starting transfers between devices  43.4 us (40%)
  blocking collectives  32.4 us (30%)
  waiting for transfers between devices  13.9 us (13%)
  Pallas kernels  12.3 us (11%)
  local copies, waits for them, and re-layouts  3.75 us (3%)
    all_to_all x1, blocking collectives, per_device(): lax.all_to_all(restored, 'chan', split_axis=0, concat_axis=0, tiled=True)  32.4 us
    ppermute x3, starting transfers between devices, per_device(): from_above.append(lax.ppermute(from_above[-1], 'row', hop(-1)))  21.7 us
    all_to_all x1, starting transfers between devices, per_device(): lax.all_to_all(sent, 'chan', split_axis=0, concat_axis=0, tiled=True)  10.2 us
    pallas_call x1, Pallas kernels, per_device(): call(product_body, packed, [smem(), *[vmem()] * 4, anywhere(), *[vmem()]...  5.82 us
    ppermute x3, starting transfers between devices, per_device(): from_below.append(lax.ppermute(from_below[-1], 'row', hop(1)))  5.76 us
    ppermute x3, waiting for transfers between devices, per_device(): from_below.append(lax.ppermute(from_below[-1], 'row', hop(1)))  5.63 us
    ppermute x3, waiting for transfers between devices, per_device(): from_above.append(lax.ppermute(from_above[-1], 'row', hop(-1)))  4.74 us
    ppermute x2, starting transfers between devices, stacked(): return [stack, lax.ppermute(stack, 'row', swap)]  3.84 us
  transfers between devices with their start and end apart: 10, of which 5 were waited for; matrix products, arithmetic and copies ran while one was open for 1% of the time, Pallas kernels for 5%

profile of v5, /device:TPU:6, one launch (start us, length us, event | category | flops | bytes accessed | tf_op | source)
XLA Modules:
  0.0 107.3 jit_solution(10898123138803077911)
XLA Ops:
  0.0 0.0 copy-start
  0.0 0.0 copy-start.1
  0.0 1.1 %copy-done.1 = bf16[1,128,2048]{2,1,0:T(8,128)(2,1)S(1)} copy-done((bf16[1,128,2048]{2,1,0:T(8,128)(2,1)S(1)}, bf16[1,128,2048]{2,1,0:T(8,128)(2,1)}, u32[]{:S(2)}) %copy-start.1) | copy-done | bytes 524312
  1.1 0.1 shard_map.55.refs_0_
  1.2 10.9 %collective-permute-start.3 = (bf16[128,1152]{1,0:T(8,128)(2,1)S(1)}, bf16[128,1152]{1,0:T(8,128)(2,1)S(1)}, u32[]{:S(2)}, u32[]{:S(2)}) collective-permute-start(bf16[128,1152]{1,0:T(8,128)(2,1)S(1)} %shard_map.55.refs_0_), channel_id=1, source_target_pairs={{0,14},{1,15},{2,0},{3,1},{4,2},{5,3},{6,4},{7,5},{8,6},{9,7},{10,... | collective-permute-start | bytes 884744 | tf_op jit(solution)/shard_map/ppermute | solution.py:207
  12.2 1.9 %collective-permute-start = (bf16[128,1152]{1,0:T(8,128)(2,1)S(1)}, bf16[128,1152]{1,0:T(8,128)(2,1)S(1)}, u32[]{:S(2)}, u32[]{:S(2)}) collective-permute-start(bf16[128,1152]{1,0:T(8,128)(2,1)S(1)} %shard_map.55.refs_0_), channel_id=1, source_target_pairs={{0,2},{1,3},{2,4},{3,5},{4,6},{5,7},{6,8},{7,9},{8,10},{9,11},{10,... | collective-permute-start | bytes 884744 | tf_op jit(solution)/shard_map/ppermute | solution.py:206
  14.1 0.0 copy-done
  14.1 1.2 %shard_map.56 = bf16[32,96,128]{2,1,0:T(8,128)(2,1)} custom-call(bf16[192,2048]{1,0:T(8,128)(2,1)S(1)} %bitcast.6), custom_call_target="tpu_custom_call" | custom-call | tf_op jit(solution)/shard_map/pallas_call | solution.py:203
  15.3 10.2 %all-to-all-start = ((bf16[32,96,128]{2,1,0:T(8,128)(2,1)}), bf16[32,96,128]{2,1,0:T(8,128)(2,1)S(1)}, u32[]{:S(2)}, u32[]{:S(2)}) async-start(bf16[32,96,128]{2,1,0:T(8,128)(2,1)} %shard_map.56), calls=%async_computation | async-start | bytes 1572864 | tf_op jit(solution)/shard_map/all_to_all | solution.py:209
  25.5 0.0 collective-permute-done.3.refs_2_
  25.5 5.1 %collective-permute-start.5 = (bf16[128,1152]{1,0:T(8,128)(2,1)S(1)}, bf16[128,1152]{1,0:T(8,128)(2,1)S(1)}, u32[]{:S(2)}, u32[]{:S(2)}) collective-permute-start(bf16[128,1152]{1,0:T(8,128)(2,1)S(1)} %collective-permute-done.3.refs_2_), channel_id=1, source_target_pairs={{0,14},{1,15},{2,0},{3,1},{4,2},{5,3},{6,4},{7,5},{8,6},{9,7},{10,... | collective-permute-start | bytes 884744 | tf_op jit(solution)/shard_map/ppermute | solution.py:207
  30.7 0.0 collective-permute-done.refs_1_
  30.7 1.9 %collective-permute-start.1 = (bf16[128,1152]{1,0:T(8,128)(2,1)S(1)}, bf16[128,1152]{1,0:T(8,128)(2,1)S(1)}, u32[]{:S(2)}, u32[]{:S(2)}) collective-permute-start(bf16[128,1152]{1,0:T(8,128)(2,1)S(1)} %collective-permute-done.refs_1_), channel_id=1, source_target_pairs={{0,2},{1,3},{2,4},{3,5},{4,6},{5,7},{6,8},{7,9},{8,10},{9,11},{10,... | collective-permute-start | bytes 884744 | tf_op jit(solution)/shard_map/ppermute | solution.py:206
  32.6 0.0 copy-start.2
  32.6 0.7 copy-done.2
  33.3 2.5 %collective-permute-done.5.refs_0_ = bf16[128,1152]{1,0:T(8,128)(2,1)S(1)} collective-permute-done((bf16[128,1152]{1,0:T(8,128)(2,1)S(1)}, bf16[128,1152]{1,0:T(8,128)(2,1)S(1)}, u32[]{:S(2)}, u32[]{:S(2)}) %collective-permute-start.5) | collective-permute-done | bytes 294944 | tf_op jit(solution)/shard_map/ppermute | solution.py:207
  35.8 5.6 %collective-permute-start.6 = (bf16[128,1152]{1,0:T(8,128)(2,1)S(1)}, bf16[128,1152]{1,0:T(8,128)(2,1)S(1)}, u32[]{:S(2)}, u32[]{:S(2)}) collective-permute-start(bf16[128,1152]{1,0:T(8,128)(2,1)S(1)} %collective-permute-done.5.refs_0_), channel_id=1, source_target_pairs={{0,14},{1,15},{2,0},{3,1},{4,2},{5,3},{6,4},{7,5},{8,6},{9,7},{10,... | collective-permute-start | bytes 884744 | tf_op jit(solution)/shard_map/ppermute | solution.py:207
  41.4 0.0 collective-permute-done.1.refs_3_
  41.4 0.0 copy-start.4
  41.4 1.9 %collective-permute-start.2 = (bf16[128,1152]{1,0:T(8,128)(2,1)S(1)}, bf16[128,1152]{1,0:T(8,128)(2,1)S(1)}, u32[]{:S(2)}, u32[]{:S(2)}) collective-permute-start(bf16[128,1152]{1,0:T(8,128)(2,1)S(1)} %collective-permute-done.1.refs_3_), channel_id=1, source_target_pairs={{0,2},{1,3},{2,4},{3,5},{4,6},{5,7},{6,8},{7,9},{8,10},{9,11},{10,... | collective-permute-start | bytes 884744 | tf_op jit(solution)/shard_map/ppermute | solution.py:206
  43.3 2.3 %collective-permute-done.6.refs_2_ = bf16[128,1152]{1,0:T(8,128)(2,1)S(1)} collective-permute-done((bf16[128,1152]{1,0:T(8,128)(2,1)S(1)}, bf16[128,1152]{1,0:T(8,128)(2,1)S(1)}, u32[]{:S(2)}, u32[]{:S(2)}) %collective-permute-start.6) | collective-permute-done | bytes 294944 | tf_op jit(solution)/shard_map/ppermute | solution.py:207
  45.6 5.6 %collective-permute-done.2.refs_1_ = bf16[128,1152]{1,0:T(8,128)(2,1)S(1)} collective-permute-done((bf16[128,1152]{1,0:T(8,128)(2,1)S(1)}, bf16[128,1152]{1,0:T(8,128)(2,1)S(1)}, u32[]{:S(2)}, u32[]{:S(2)}) %collective-permute-start.2) | collective-permute-done | bytes 294944 | tf_op jit(solution)/shard_map/ppermute | solution.py:206
  51.2 0.7 broadcast_select_fusion
  52.0 1.9 %collective-permute-start.7 = (bf16[128,1152]{1,0:T(8,128)(2,1)}, bf16[128,1152]{1,0:T(8,128)(2,1)}, u32[]{:S(2)}, u32[]{:S(2)}) collective-permute-start(bf16[128,1152]{1,0:T(8,128)(2,1)} %broadcast_select_fusion), channel_id=1, source_target_pairs={{0,2},{1,15},{2,4},{3,1},{4,6},{5,3},{6,8},{7,5},{8,10},{9,7},{10,... | collective-permute-start | bytes 884744 | tf_op jit(solution)/shard_map/ppermute | solution.py:212
  54.5 0.0 copy-done.4
  54.5 0.0 copy-start.3
  54.6 1.0 copy-done.3
  55.5 0.0 copy-start.5
  55.5 1.0 copy-done.5
  56.5 0.0 copy-start.6
  56.5 0.0 copy-start.7
  56.5 0.1 shard_map.58.refs_0_
  56.6 1.9 %collective-permute-start.4 = (bf16[512,1152]{1,0:T(8,128)(2,1)S(1)}, bf16[512,1152]{1,0:T(8,128)(2,1)}, u32[]{:S(2)}, u32[]{:S(2)}) collective-permute-start(bf16[512,1152]{1,0:T(8,128)(2,1)S(1)} %shard_map.58.refs_0_), channel_id=1, source_target_pairs={{0,1},{1,0},{2,3},{3,2},{4,5},{5,4},{6,7},{7,6},{8,9},{9,8},{10,11... | collective-permute-start | bytes 3538952 | tf_op jit(solution)/shard_map/ppermute | solution.py:232
  58.5 0.0 all-to-all-done.groups_ref
  58.5 0.0 copy-done.6
  58.5 0.0 copy-done.7
  58.5 2.8 %shard_map.57 = (bf16[192,2048]{1,0:T(8,128)(2,1)S(1)}, s32[1,2048]{1,0:T(1,128)S(1)}, f32[1,2048]{1,0:T(1,128)S(1)}) custom-call(s32[1]{0:T(128)S(6)} %sub.7.live_ref, s32[1]{0:T(128)} %bitcast.1.row_ref, bf16[32,96,128]{2,1,0:T(8,128)(2,1)S(1)} %all-to-all-done.groups_ref, s32[1,2048]{1,0:T(1,128)S(1)} %copy-done.6, f32[1,2048]{1,0:T(1,128)S(1)} %copy-done.7), custom_call_target="tpu_custom_call" | custom-call | tf_op jit(solution)/shard_map/pallas_call | solution.py:214
  61.4 0.7 collective-permute-done.7.refs_3_
  62.1 1.0 shard_map.59.refs_2_
  63.2 1.9 %collective-permute-start.8 = (bf16[512,1152]{1,0:T(8,128)(2,1)S(1)}, bf16[512,1152]{1,0:T(8,128)(2,1)S(1)}, u32[]{:S(2)}, u32[]{:S(2)}) collective-permute-start(bf16[512,1152]{1,0:T(8,128)(2,1)S(1)} %shard_map.59.refs_2_), channel_id=1, source_target_pairs={{0,1},{1,0},{2,3},{3,2},{4,5},{5,4},{6,7},{7,6},{8,9},{9,8},{10,11... | collective-permute-start | bytes 3538952 | tf_op jit(solution)/shard_map/ppermute | solution.py:232
  65.1 0.0 collective-permute-done.4.refs_1_
  65.1 2.8 %collective-permute-done.8.refs_3_ = bf16[512,1152]{1,0:T(8,128)(2,1)S(1)} collective-permute-done((bf16[512,1152]{1,0:T(8,128)(2,1)S(1)}, bf16[512,1152]{1,0:T(8,128)(2,1)S(1)}, u32[]{:S(2)}, u32[]{:S(2)}) %collective-permute-start.8) | collective-permute-done | bytes 1179680 | tf_op jit(solution)/shard_map/ppermute | solution.py:232
  67.9 5.8 %shard_map.60 = bf16[32,96,128]{2,1,0:T(8,128)(2,1)S(1)} custom-call(s32[1]{0:T(128)} %bitcast.core_ref, bf16[192,2048]{1,0:T(8,128)(2,1)S(1)} %get-tuple-element.11.recoupled_ref, s32[1,2048]{1,0:T(1,128)S(1)} %get-tuple-element.12.order_ref, f32[1,2048]{1,0:T(1,128)S(1)} %get-tuple-element.13.weight_ref, bf16[512,1152]{1,0:T(8,128)(2,1)S(1)} %shard_map.58.refs_0_, ...), custom_call_target="tpu_custom_call" | custom-call | tf_op jit(solution)/shard_map/pallas_call | solution.py:236
  73.7 32.4 %all_to_all.10.groups_ref = bf16[32,96,128]{2,1,0:T(8,128)(2,1)S(1)} all-to-all(bf16[32,96,128]{2,1,0:T(8,128)(2,1)S(1)} %shard_map.60), channel_id=1, replica_groups=mesh['chan'=32,'row'=16] {'chan'}, dimensions={0} | all-to-all | bytes 1572864 | tf_op jit(solution)/shard_map/all_to_all | solution.py:248
  106.1 1.2 %shard_map.61 = bf16[192,2048]{1,0:T(8,128)(2,1)} custom-call(bf16[32,96,128]{2,1,0:T(8,128)(2,1)S(1)} %all_to_all.10.groups_ref), custom_call_target="tpu_custom_call" | custom-call | tf_op jit(solution)/shard_map/pallas_call | solution.py:249
Async XLA Ops:
  0.0 14.1 %copy-start = (bf16[1,192,2048]{2,1,0:T(8,128)(2,1)S(1)}, bf16[1,192,2048]{2,1,0:T(8,128)(2,1)}, u32[]{:S(2)}) copy-start(bf16[1,192,2048]{2,1,0:T(8,128)(2,1)} %param.5) | copy-start | bytes 2359300
  0.0 1.1 %copy-start.1 = (bf16[1,128,2048]{2,1,0:T(8,128)(2,1)S(1)}, bf16[1,128,2048]{2,1,0:T(8,128)(2,1)}, u32[]{:S(2)}) copy-start(bf16[1,128,2048]{2,1,0:T(8,128)(2,1)} %param.6) | copy-start | bytes 1572868
  1.2 24.3 %collective-permute-start.3 = (bf16[128,1152]{1,0:T(8,128)(2,1)S(1)}, bf16[128,1152]{1,0:T(8,128)(2,1)S(1)}, u32[]{:S(2)}, u32[]{:S(2)}) collective-permute-start(bf16[128,1152]{1,0:T(8,128)(2,1)S(1)} %shard_map.55.refs_0_), channel_id=1, source_target_pairs={{0,14},{1,15},{2,0},{3,1},{4,2},{5,3},{6,4},{7,5},{8,6},{9,7},{10,... | collective-permute-start | bytes 884744 | tf_op jit(solution)/shard_map/ppermute | solution.py:207
  12.2 18.5 %collective-permute-start = (bf16[128,1152]{1,0:T(8,128)(2,1)S(1)}, bf16[128,1152]{1,0:T(8,128)(2,1)S(1)}, u32[]{:S(2)}, u32[]{:S(2)}) collective-permute-start(bf16[128,1152]{1,0:T(8,128)(2,1)S(1)} %shard_map.55.refs_0_), channel_id=1, source_target_pairs={{0,2},{1,3},{2,4},{3,5},{4,6},{5,7},{6,8},{7,9},{8,10},{9,11},{10,... | collective-permute-start | bytes 884744 | tf_op jit(solution)/shard_map/ppermute | solution.py:206
  15.3 43.2 %all-to-all-start = ((bf16[32,96,128]{2,1,0:T(8,128)(2,1)}), bf16[32,96,128]{2,1,0:T(8,128)(2,1)S(1)}, u32[]{:S(2)}, u32[]{:S(2)}) async-start(bf16[32,96,128]{2,1,0:T(8,128)(2,1)} %shard_map.56), calls=%async_computation | async-start | bytes 1572864 | tf_op jit(solution)/shard_map/all_to_all | solution.py:209
  25.5 10.3 %collective-permute-start.5 = (bf16[128,1152]{1,0:T(8,128)(2,1)S(1)}, bf16[128,1152]{1,0:T(8,128)(2,1)S(1)}, u32[]{:S(2)}, u32[]{:S(2)}) collective-permute-start(bf16[128,1152]{1,0:T(8,128)(2,1)S(1)} %collective-permute-done.3.refs_2_), channel_id=1, source_target_pairs={{0,14},{1,15},{2,0},{3,1},{4,2},{5,3},{6,4},{7,5},{8,6},{9,7},{10,... | collective-permute-start | bytes 884744 | tf_op jit(solution)/shard_map/ppermute | solution.py:207
  30.7 10.7 %collective-permute-start.1 = (bf16[128,1152]{1,0:T(8,128)(2,1)S(1)}, bf16[128,1152]{1,0:T(8,128)(2,1)S(1)}, u32[]{:S(2)}, u32[]{:S(2)}) collective-permute-start(bf16[128,1152]{1,0:T(8,128)(2,1)S(1)} %collective-permute-done.refs_1_), channel_id=1, source_target_pairs={{0,2},{1,3},{2,4},{3,5},{4,6},{5,7},{6,8},{7,9},{8,10},{9,11},{10,... | collective-permute-start | bytes 884744 | tf_op jit(solution)/shard_map/ppermute | solution.py:206
  32.6 0.7 copy-start.2
  35.8 9.8 %collective-permute-start.6 = (bf16[128,1152]{1,0:T(8,128)(2,1)S(1)}, bf16[128,1152]{1,0:T(8,128)(2,1)S(1)}, u32[]{:S(2)}, u32[]{:S(2)}) collective-permute-start(bf16[128,1152]{1,0:T(8,128)(2,1)S(1)} %collective-permute-done.5.refs_0_), channel_id=1, source_target_pairs={{0,14},{1,15},{2,0},{3,1},{4,2},{5,3},{6,4},{7,5},{8,6},{9,7},{10,... | collective-permute-start | bytes 884744 | tf_op jit(solution)/shard_map/ppermute | solution.py:207
  41.4 13.2 %copy-start.4 = (bf16[128,1152]{1,0:T(8,128)(2,1)}, bf16[128,1152]{1,0:T(8,128)(2,1)S(1)}, u32[]{:S(2)}) copy-start(bf16[128,1152]{1,0:T(8,128)(2,1)S(1)} %collective-permute-done.1.refs_3_) | copy-start | bytes 884740
  41.4 9.8 %collective-permute-start.2 = (bf16[128,1152]{1,0:T(8,128)(2,1)S(1)}, bf16[128,1152]{1,0:T(8,128)(2,1)S(1)}, u32[]{:S(2)}, u32[]{:S(2)}) collective-permute-start(bf16[128,1152]{1,0:T(8,128)(2,1)S(1)} %collective-permute-done.1.refs_3_), channel_id=1, source_target_pairs={{0,2},{1,3},{2,4},{3,5},{4,6},{5,7},{6,8},{7,9},{8,10},{9,11},{10,... | collective-permute-start | bytes 884744 | tf_op jit(solution)/shard_map/ppermute | solution.py:206
  52.0 10.1 %collective-permute-start.7 = (bf16[128,1152]{1,0:T(8,128)(2,1)}, bf16[128,1152]{1,0:T(8,128)(2,1)}, u32[]{:S(2)}, u32[]{:S(2)}) collective-permute-start(bf16[128,1152]{1,0:T(8,128)(2,1)} %broadcast_select_fusion), channel_id=1, source_target_pairs={{0,2},{1,15},{2,4},{3,1},{4,6},{5,3},{6,8},{7,5},{8,10},{9,7},{10,... | collective-permute-start | bytes 884744 | tf_op jit(solution)/shard_map/ppermute | solution.py:212
  54.5 1.0 copy-start.3
  55.5 1.0 copy-start.5
  56.5 2.0 %copy-start.6 = (s32[1,2048]{1,0:T(1,128)S(1)}, s32[1,2048]{1,0:T(1,128)}, u32[]{:S(2)}) copy-start(s32[1,2048]{1,0:T(1,128)} %order_in.1) | copy-start | bytes 24580
  56.5 2.0 %copy-start.7 = (f32[1,2048]{1,0:T(1,128)S(1)}, f32[1,2048]{1,0:T(1,128)}, u32[]{:S(2)}) copy-start(f32[1,2048]{1,0:T(1,128)} %weight_in.1) | copy-start | bytes 24580
  56.6 8.5 %collective-permute-start.4 = (bf16[512,1152]{1,0:T(8,128)(2,1)S(1)}, bf16[512,1152]{1,0:T(8,128)(2,1)}, u32[]{:S(2)}, u32[]{:S(2)}) collective-permute-start(bf16[512,1152]{1,0:T(8,128)(2,1)S(1)} %shard_map.58.refs_0_), channel_id=1, source_target_pairs={{0,1},{1,0},{2,3},{3,2},{4,5},{5,4},{6,7},{7,6},{8,9},{9,8},{10,11... | collective-permute-start | bytes 3538952 | tf_op jit(solution)/shard_map/ppermute | solution.py:232
  63.2 4.7 %collective-permute-start.8 = (bf16[512,1152]{1,0:T(8,128)(2,1)S(1)}, bf16[512,1152]{1,0:T(8,128)(2,1)S(1)}, u32[]{:S(2)}, u32[]{:S(2)}) collective-permute-start(bf16[512,1152]{1,0:T(8,128)(2,1)S(1)} %shard_map.59.refs_2_), channel_id=1, source_target_pairs={{0,1},{1,0},{2,3},{3,2},{4,5},{5,4},{6,7},{7,6},{8,9},{9,8},{10,11... | collective-permute-start | bytes 3538952 | tf_op jit(solution)/shard_map/ppermute | solution.py:232
